TPU v7x, 32 devices: a whole 2x2x4 slice. The times are simulated.
32 devices in a mesh: dp: 8 (over z, x), grp: 4 (over y, core).
Axes of the slice: x: 2, y: 2, z: 4, core: 2. Of those that a mesh axis runs over, the one named last changes fastest.
Arguments:
- queries: bfloat16 [2048, 4096], P('dp', 'grp'), may hold values from -6 to 6
- passages: bfloat16 [16, 128, 4096], P(None, 'dp', 'grp'), may hold values from -6 to 6
- block_lists: int32 [16, 3], P('dp'), may hold values from 0 to 15
- list_lengths: int32 [16], P('dp'), may hold values from 1 to 3, as said below
- positive: int32 [2048], P('dp'), may hold values from 0 to 2047, as said below
- loss_grad: float32 [2048], P('dp'), may hold values from -16 to 16
Outputs:
- losses: float32 [2048], P('dp')
- grad_queries: bfloat16 [2048, 4096], P('dp', 'grp')
- grad_passages: bfloat16 [16, 128, 4096], P(None, 'dp', 'grp')
Inputs may be any that keep to these rules, and one draw needn't show every extreme that they name: `block_lists`: entries of a list past its length are ignored. `list_lengths`: the 2 query blocks of one dp index list 4 blocks or fewer together; in every draw some dp index lists exactly 4, with one of its blocks listing 3. positive[q] = n * 128 + r with r // 16 == q // 256.
All inputs are finite; a program needn't handle non-finite values.
Results may differ from a plain program's by a relative error of at most 0.0052.
Values may be sent and summed in bfloat16 or wider, within the bound.
No kernel may reach another device: no remote copies, remote signals or barrier semaphores. Data moves between devices by JAX's collectives and lax.ppermute only.
A program may use at most 64 MiB of HBM per device.

v0:
```python
import math

import jax
import jax.numpy as jnp
from jax import lax
from jax.sharding import PartitionSpec as P

D = 4096
LIVE_MAX = 4


def pick_rows(selector, table):
    return jnp.sum(jnp.where(selector[:, :, None], table[None], 0.0), axis=1)


def per_device(queries, passages, block_lists, list_lengths, positive, loss_grad):
    score_scale = 3.0 / math.sqrt(D)
    dp_count = lax.axis_size("dp")
    dp_owner = lax.axis_index("dp")
    block_count, list_cap = block_lists.shape
    block_total, shard_rows, feature_width = passages.shape
    block_size = shard_rows * dp_count
    query_rows = queries.shape[0]
    query_blocks = queries.reshape(block_count, block_size, feature_width)
    entry_index = jnp.arange(list_cap, dtype=jnp.int32)
    block_index = jnp.arange(block_count, dtype=jnp.int32)
    slot_count = LIVE_MAX
    slot_index = jnp.arange(slot_count, dtype=jnp.int32)
    list_ends = jnp.cumsum(list_lengths)
    list_starts = list_ends - list_lengths
    slot_block = jnp.minimum(
        jnp.sum((list_ends[None, :] <= slot_index[:, None]).astype(jnp.int32), axis=1),
        block_count - 1,
    )
    owner_match = slot_block[:, None] == block_index[None, :]
    offset = slot_index - jnp.sum(jnp.where(owner_match, list_starts[None, :], 0), axis=1)
    slot_live = slot_index < list_ends[block_count - 1]
    entry_match = owner_match[:, :, None] & (offset[:, None, None] == entry_index[None, None, :])
    slot_ids = jnp.sum(jnp.where(entry_match, block_lists[None], 0), axis=(1, 2))
    all_ids = lax.all_gather(slot_ids, "dp", axis=0, tiled=True)
    outgoing = passages[all_ids].reshape(dp_count, slot_count, shard_rows, feature_width)
    fetched = lax.all_to_all(outgoing, "dp", split_axis=0, concat_axis=2, tiled=True).reshape(
        slot_count, block_size, feature_width
    )
    local_rows = passages.reshape(block_total * shard_rows, feature_width)
    block_match = slot_block[:, None] == block_index[None, :]
    chosen = jnp.einsum(
        "sb,bqf->sqf",
        block_match.astype(jnp.bfloat16),
        query_blocks,
        preferred_element_type=jnp.float32,
    ).astype(jnp.bfloat16)
    part_in = lax.dot_general(
        queries, local_rows, (((1,), (1,)), ((), ())), preferred_element_type=jnp.float32
    )
    part_list = jnp.einsum("sqf,spf->sqp", chosen, fetched, preferred_element_type=jnp.float32)
    full_in, full_list = lax.psum((part_in, part_list), "grp")
    scores_in = score_scale * full_in
    scores_list = score_scale * full_list
    slot_open = block_match & slot_live[:, None]
    slot_peak = jnp.max(scores_list, axis=2)
    list_peak = jnp.max(
        jnp.where(slot_open[:, :, None], slot_peak[:, None, :], -jnp.inf), axis=0
    ).reshape(query_rows)
    row_peak = jnp.maximum(jnp.max(scores_in, axis=1), list_peak)
    slot_shift = pick_rows(block_match, row_peak.reshape(block_count, block_size))
    slot_sums = jnp.sum(jnp.exp(scores_list - slot_shift[:, :, None]), axis=2)
    list_total = jnp.sum(
        jnp.where(slot_open[:, :, None], slot_sums[:, None, :], 0.0), axis=0
    ).reshape(query_rows)
    row_total = jnp.sum(jnp.exp(scores_in - row_peak[:, None]), axis=1) + list_total
    log_total = row_peak + jnp.log(row_total)
    pos_column = positive // block_size * shard_rows + positive % block_size - dp_owner * shard_rows
    column_index = jnp.arange(block_total * shard_rows, dtype=jnp.int32)
    is_positive = column_index[None, :] == pos_column[:, None]
    positive_score = jnp.sum(jnp.where(is_positive, scores_in, 0.0), axis=1)
    losses = log_total - positive_score
    weights_in = (
        loss_grad[:, None]
        * (jnp.exp(scores_in - log_total[:, None]) - is_positive.astype(jnp.float32))
    ).astype(jnp.bfloat16)
    slot_log = pick_rows(block_match, log_total.reshape(block_count, block_size))
    slot_grad = pick_rows(block_match, loss_grad.reshape(block_count, block_size))
    weights_list = jnp.where(
        slot_live[:, None, None],
        slot_grad[:, :, None] * jnp.exp(scores_list - slot_log[:, :, None]),
        0.0,
    ).astype(jnp.bfloat16)
    near_terms = jnp.dot(weights_in, local_rows, preferred_element_type=jnp.float32)
    per_slot = jnp.einsum("sqp,spf->sqf", weights_list, fetched, preferred_element_type=jnp.float32)
    far_terms = jnp.einsum(
        "sb,sqf->bqf", block_match.astype(jnp.float32), per_slot, precision=lax.Precision.HIGHEST
    ).reshape(query_rows, feature_width)
    grad_queries = (score_scale * (near_terms + far_terms)).astype(jnp.bfloat16)
    shares = (
        score_scale
        * jnp.einsum("sqp,sqf->spf", weights_list, chosen, preferred_element_type=jnp.float32)
    ).astype(jnp.bfloat16)
    returned = lax.all_to_all(
        shares.reshape(1, slot_count, block_size, feature_width),
        "dp",
        split_axis=2,
        concat_axis=0,
        tiled=True,
    )
    own_part = score_scale * lax.dot_general(
        weights_in, queries, (((0,), (0,)), ((), ())), preferred_element_type=jnp.float32
    )
    summed = (
        own_part.reshape(block_total, shard_rows, feature_width)
        .at[all_ids]
        .add(returned.reshape(dp_count * slot_count, shard_rows, feature_width).astype(jnp.float32))
    )
    return (losses, grad_queries, summed.astype(jnp.bfloat16))


def solution(mesh):
    in_specs = (P("dp", "grp"), P(None, "dp", "grp"), P("dp", None), P("dp"), P("dp"), P("dp"))
    out_specs = (P("dp"), P("dp", "grp"), P(None, "dp", "grp"))
    return jax.shard_map(
        per_device, mesh=mesh, in_specs=in_specs, out_specs=out_specs, check_vma=False
    )
```

profile of v0, /device:TPU:0, one launch (start us, length us, event | category | flops | bytes accessed | tf_op | source)
XLA Modules:
  0.0 145.7 jit_solution(18238357606578402877)
XLA Ops:
  7.2 0.9 reduce-window.4
  10.9 1.2 dynamic-slice
  13.2 13.1 %all-reduce = s32[32]{0:T(128)S(1)} all-reduce(s32[32]{0:T(128)S(1)} %dynamic-update-slice), channel_id=1, replica_groups=mesh['dp'=8,'grp'=4] {'dp'}, use_global_device_ids=true, to_apply=%add | all-reduce | flops 32 | bytes 256
  26.3 2.8 %gather_fusion = bf16[32,16,1024]{2,1,0:T(8,128)(2,1)} fusion(bf16[16,16,1024]{2,1,0:T(8,128)(2,1)} %param.7, s32[1024]{0:T(1024)S(1)} %pad_clamp_fusion), kind=kCustom, calls=%fused_computation | custom fusion | bytes 2097280 | tf_op jit(solution)/shard_map/gather | solution.py:41
  29.0 3.6 %all-to-all-start = ((bf16[8,4,16,1024]{3,2,1,0:T(8,128)(2,1)}), bf16[8,4,16,1024]{3,2,1,0:T(8,128)(2,1)S(1)}, u32[]{:S(2)}, u32[]{:S(2)}) async-start(bf16[8,4,16,1024]{3,2,1,0:T(8,128)(2,1)} %bitcast.7), calls=%async_computation | async-start | bytes 2097152 | tf_op jit(solution)/shard_map/all_to_all | solution.py:42
  32.7 1.0 fusion.22
  33.7 1.9 %convolution_convert_fusion = bf16[4,128,1024]{2,0,1:T(4,128)(2,1)} fusion(bf16[2,128,1024]{2,1,0:T(8,128)(2,1)S(1)} %bitcast.52, s32[4]{0:T(128)S(1)} %broadcast_minimum_fusion), kind=kOutput, calls=%fused_computation.6 | convolution fusion | flops 2621448 | bytes 1572880 | tf_op jit(solution)/shard_map/sb,bqf->sqf/dot_general | solution.py:47
  35.6 20.2 %all-to-all-done = bf16[8,4,16,1024]{3,2,1,0:T(8,128)(2,1)S(1)} async-done(((bf16[8,4,16,1024]{3,2,1,0:T(8,128)(2,1)}), bf16[8,4,16,1024]{3,2,1,0:T(8,128)(2,1)S(1)}, u32[]{:S(2)}, u32[]{:S(2)}) %all-to-all-start) | async-done | bytes 1048608 | tf_op jit(solution)/shard_map/all_to_all | solution.py:42
  56.0 1.1 copy-done.4
  57.1 1.3 fusion.6
  58.4 32.5 %all-reduce.4.cloned.1.call-done = (f32[256,256]{1,0:T(8,128)}, f32[4,128,128]{2,1,0:T(8,128)}) async-done(((f32[256,256]{1,0:T(8,128)}, f32[4,128,128]{2,1,0:T(8,128)}), (f32[256,256]{1,0:T(8,128)}, f32[4,128,128]{2,1,0:T(8,128)})) %all-reduce.4.cloned.1.call-update) | async-done | bytes 524304 | tf_op jit(solution)/shard_map/psum | solution.py:57
  90.9 1.1 multiply_reduce_fusion.1
  92.0 1.1 multiply_reduce_fusion
  93.3 1.2 exponential_reduce_fusion
  94.6 1.2 select_reduce_fusion
  95.9 1.9 %fusion.2 = bf16[1,4,128,1024]{3,2,1,0:T(8,128)(2,1)S(1)} fusion(bf16[4,128,1024]{2,0,1:T(4,128)(2,1)S(1)} %copy-done.5, f32[4,128,128]{2,1,0:T(8,128)} %get-tuple-element.8, f32[4,128]{1,0:T(4,128)S(1)} %get-tuple-element.6, f32[4,128]{1,0:T(4,128)S(1)} %get-tuple-element.5, pred[4]{0:T(512)(128)(4,1)S(1)} %iota_compare_fusion.3), kind=kOutput, calls=%fused_computation.7 | convolution fusion | flops 135593984 | bytes 2363396 | tf_op jit(solution)/shard_map/sqp,sqf->spf/dot_general | solution.py:97
  97.8 1.8 %copy.49 = bf16[1,4,128,1024]{3,1,0,2:T(4,128)(2,1)} copy(bf16[1,4,128,1024]{3,2,1,0:T(8,128)(2,1)S(1)} %fusion.2) | data formatting | bytes 2097152 | tf_op jit(solution)/shard_map/reshape | solution.py:100
  99.6 5.5 %all-to-all-start.1 = ((bf16[1,4,128,1024]{3,1,0,2:T(4,128)(2,1)}), bf16[1,4,128,1024]{3,1,0,2:T(4,128)(2,1)S(1)}, u32[]{:S(2)}, u32[]{:S(2)}) async-start(bf16[1,4,128,1024]{3,1,0,2:T(4,128)(2,1)} %copy.49), calls=%async_computation.1 | async-start | bytes 2097152 | tf_op jit(solution)/shard_map/all_to_all | solution.py:99
  105.6 3.2 %fusion = f32[2,128,1024]{2,0,1:T(2,128)S(1)} fusion(f32[4,128,1024]{2,1,0:T(8,128)S(1)} %fusion.19, s32[4]{0:T(128)S(1)} %broadcast_minimum_fusion), kind=kOutput, calls=%fused_computation.3 | convolution fusion | flops 12582920 | bytes 3145744 | tf_op jit(solution)/shard_map/sb,sqf->bqf/dot_general | solution.py:91
  110.3 1.2 fusion.4
  111.5 18.7 %all-to-all-done.1 = bf16[1,4,128,1024]{3,1,0,2:T(4,128)(2,1)S(1)} async-done(((bf16[1,4,128,1024]{3,1,0,2:T(4,128)(2,1)}), bf16[1,4,128,1024]{3,1,0,2:T(4,128)(2,1)S(1)}, u32[]{:S(2)}, u32[]{:S(2)}) %all-to-all-start.1) | async-done | bytes 1048608 | tf_op jit(solution)/shard_map/all_to_all | solution.py:99
  130.8 2.6 %copy.50 = f32[8,1,4,16,1024]{4,3,2,0,1:T(8,128)} copy(f32[8,1,4,16,1024]{4,2,3,0,1:T(4,128)S(1)} %convert_bitcast_fusion) | data formatting | bytes 4194304 | tf_op jit(solution)/shard_map/convert_element_type | solution.py:112
  133.4 4.7 %scatter_fusion = f32[16,16,1024]{2,1,0:T(8,128)S(1)} fusion(f32[16,16,1024]{2,1,0:T(8,128)S(1)} %bitcast.53, s32[32]{0:T(128)S(1)} %compare_select_fusion, f32[32,16,1024]{2,1,0:T(8,128)} %bitcast.54), kind=kCustom, calls=%fused_computation.1 | custom fusion | flops 524288 | bytes 6291584 | tf_op jit(solution)/shard_map/scatter-add | solution.py:112
  138.0 0.9 convert_element_type.49
  (46 shorter events, 6.3 us)
Async XLA Ops:
  7.2 25.5 %copy-start = (bf16[256,1024]{1,0:T(8,128)(2,1)S(1)}, bf16[256,1024]{1,0:T(8,128)(2,1)}, u32[]{:S(2)}) copy-start(bf16[256,1024]{1,0:T(8,128)(2,1)} %param.6) | copy-start | bytes 1572868
  26.3 6.4 %copy-start.1 = (bf16[16,16,1024]{2,1,0:T(8,128)(2,1)S(1)}, bf16[16,16,1024]{2,1,0:T(8,128)(2,1)}, u32[]{:S(2)}) copy-start(bf16[16,16,1024]{2,1,0:T(8,128)(2,1)} %param.7) | copy-start | bytes 1572868
  29.0 26.8 %all-to-all-start = ((bf16[8,4,16,1024]{3,2,1,0:T(8,128)(2,1)}), bf16[8,4,16,1024]{3,2,1,0:T(8,128)(2,1)S(1)}, u32[]{:S(2)}, u32[]{:S(2)}) async-start(bf16[8,4,16,1024]{3,2,1,0:T(8,128)(2,1)} %bitcast.7), calls=%async_computation | async-start | bytes 2097152 | tf_op jit(solution)/shard_map/all_to_all | solution.py:42
  32.6 58.3 %all-reduce.4.cloned.1.call-start = ((), (), s32[]{:S(2)}) async-start(), calls=%async_computation.2 | async-start | bytes 1048576 | tf_op jit(solution)/shard_map/psum | solution.py:57
  55.9 1.2 copy-start.4
  55.9 2.5 %copy-start.7 = (s32[256]{0:T(256)S(1)}, s32[256]{0:T(256)}, u32[]{:S(2)}) copy-start(s32[256]{0:T(256)} %param.10) | copy-start | bytes 3076
  56.0 39.8 %copy-start.6 = (f32[256]{0:T(256)S(1)}, f32[256]{0:T(256)}, u32[]{:S(2)}) copy-start(f32[256]{0:T(256)} %param.11) | copy-start | bytes 3076
  56.0 39.9 %copy-start.5 = (bf16[4,128,1024]{2,0,1:T(4,128)(2,1)S(1)}, bf16[4,128,1024]{2,0,1:T(4,128)(2,1)}, u32[]{:S(2)}) copy-start(bf16[4,128,1024]{2,0,1:T(4,128)(2,1)} %convolution_convert_fusion) | copy-start | bytes 3145732
  97.8 7.3 %copy-start.3 = (f32[4,128,128]{2,1,0:T(8,128)S(1)}, f32[4,128,128]{2,1,0:T(8,128)}, u32[]{:S(2)}) copy-start(f32[4,128,128]{2,1,0:T(8,128)} %get-tuple-element.8) | copy-start | bytes 786436
  99.6 30.6 %all-to-all-start.1 = ((bf16[1,4,128,1024]{3,1,0,2:T(4,128)(2,1)}), bf16[1,4,128,1024]{3,1,0,2:T(4,128)(2,1)S(1)}, u32[]{:S(2)}, u32[]{:S(2)}) async-start(bf16[1,4,128,1024]{3,1,0,2:T(4,128)(2,1)} %copy.49), calls=%async_computation.1 | async-start | bytes 2097152 | tf_op jit(solution)/shard_map/all_to_all | solution.py:99
  105.6 4.2 %copy-start.2 = (f32[256,256]{1,0:T(8,128)S(1)}, f32[256,256]{1,0:T(8,128)}, u32[]{:S(2)}) copy-start(f32[256,256]{1,0:T(8,128)} %get-tuple-element.7) | copy-start | bytes 786436
Sparse Core Ops, SparseCore 0:
  58.5 32.3 all-reduce.3
where the time goes:
time: 146 us
  waiting for transfers between devices  71.5 us (49%)
  between operations  14.9 us (10%)
  other arithmetic  14.1 us (10%)
  blocking collectives  13.1 us (9%)
  local copies, waits for them, and re-layouts  11.5 us (8%)
  matrix products  11.5 us (8%)
  starting transfers between devices  9.11 us (6%)
    psum x1, waiting for transfers between devices, per_device(): full_in, full_list = lax.psum((part_in, part_list), 'grp')  32.5 us
    all_to_all x1, waiting for transfers between devices, per_device(): lax.all_to_all(outgoing, 'dp', split_axis=0, concat_axis=2, tiled=True)  20.2 us
    all_to_all x1, waiting for transfers between devices, per_device(): lax.all_to_all(shares.reshape(1, slot_count, block_size, feature_width),...  18.7 us
    unnamed x1, blocking collectives  13.1 us
    all_to_all x1, starting transfers between devices, per_device(): lax.all_to_all(shares.reshape(1, slot_count, block_size, feature_width),...  5.51 us
    scatter-add x1, other arithmetic, per_device(): summed = own_part.reshape(block_total, shard_rows, feature_width).at[all_...  4.67 us
    all_to_all x1, starting transfers between devices, per_device(): lax.all_to_all(outgoing, 'dp', split_axis=0, concat_axis=2, tiled=True)  3.56 us
    unnamed x20, local copies, waits for them, and re-layouts  3.38 us
  transfers between devices with their start and end apart: 3, of which 3 were waited for; matrix products, arithmetic and copies ran while one was open for 6% of the time, Pallas kernels for 0%

commit v1 on v0

--- a/solution.py
+++ b/solution.py
@@ -1,9 +1,13 @@
+import functools
 import math
 
 import jax
 import jax.numpy as jnp
 from jax import lax
+from jax.experimental import pallas as pl
+from jax.experimental.pallas import tpu as pltpu
 from jax.sharding import PartitionSpec as P
+
 
 D = 4096
 LIVE_MAX = 4
@@ -13,7 +17,7 @@
     return jnp.sum(jnp.where(selector[:, :, None], table[None], 0.0), axis=1)
 
 
-def per_device(queries, passages, block_lists, list_lengths, positive, loss_grad):
+def exchange_plan(queries, passages, block_lists, list_lengths, positive, loss_grad):
     score_scale = 3.0 / math.sqrt(D)
     dp_count = lax.axis_size("dp")
     dp_owner = lax.axis_index("dp")
@@ -114,6 +118,429 @@
     return (losses, grad_queries, summed.astype(jnp.bfloat16))
 
 
+LOANS = (2, 1, 1)
+KERNEL_VMEM = 8 * 1024 * 1024
+NT = (((1,), (1,)), ((), ()))
+TN = (((0,), (0,)), ((), ()))
+NN = (((1,), (0,)), ((), ()))
+
+
+def power_of_two(count):
+    return count > 0 and count & (count - 1) == 0
+
+
+def mirror_fits(passage_shape):
+    dp_count, grp_count = lax.axis_size("dp"), lax.axis_size("grp")
+    block_total, shard_rows, feature_width = passage_shape
+    block_size = shard_rows * dp_count
+    return (
+        power_of_two(dp_count)
+        and dp_count > 2
+        and power_of_two(grp_count)
+        and grp_count > 1
+        and shard_rows % 16 == 0
+        and block_size % 128 == 0
+        and feature_width % 128 == 0
+        and (block_total * shard_rows) % 256 == 0
+        and block_total <= 4 * LIVE_MAX
+        and block_total % 4 == 0
+        and sum(LOANS) == LIVE_MAX
+    )
+
+
+def swap(value, axis, bit, takes_part=lambda i: True):
+    pairs = [(i, i ^ bit) for i in range(lax.axis_size(axis)) if takes_part(i)]
+    return lax.ppermute(value, axis, pairs)
+
+
+def inner(i):
+    half = lax.axis_size("dp") // 2
+    return (i // half + i // (half // 2)) % 2 == 1
+
+
+def far_rows(sources, at):
+    near, far = (source[at, :] for source in sources)
+    return jnp.where(inner(lax.axis_index("dp")), near, far)
+
+
+def swap_shared(value, bit):
+    dp_count, grp_count = lax.axis_size("dp"), lax.axis_size("grp")
+    pairs = [
+        (d * grp_count + g, (d ^ bit) * grp_count + (g ^ 1))
+        for d in range(dp_count)
+        for g in range(grp_count)
+    ]
+    return lax.ppermute(value, ("dp", "grp"), pairs)
+
+
+def sum_over_grp(keep, send):
+    half = add(keep, swap(send, "grp", 1))
+    bit = 2
+    while bit < lax.axis_size("grp"):
+        half = add(half, swap(half, "grp", bit))
+        bit *= 2
+    return half, swap(half, "grp", 1)
+
+
+def add_kernel(a, b, out):
+    out[...] = a[...] + b[...]
+
+
+def add(a, b):
+    return local_call(add_kernel, [(a.shape, a.dtype)])(a, b)[0]
+
+
+def join_kernel(a, b, out):
+    for i in range(a.shape[0]):
+        out[i] = a[i]
+        out[a.shape[0] + i] = b[i]
+
+
+def dot(a, b, dims=NN):
+    return lax.dot_general(a, b, dims, preferred_element_type=jnp.float32)
+
+
+class Lists:
+    def __init__(self, table, block_count, list_cap, slots):
+        self.table, self.block_count, self.list_cap = table, block_count, list_cap
+        self.slots = slots
+
+    def slot(self, side, s):
+        base = side * self.block_count * (1 + self.list_cap)
+        end, start, block, live = 0, 0, 0, False
+        for b in range(self.block_count):
+            begin = end
+            end = end + self.table[base + b]
+            inside = s >= begin
+            block = jnp.where(inside, b, block)
+            start = jnp.where(inside, begin, start)
+            live = s < end
+        entry = jnp.minimum(s - start, self.list_cap - 1)
+        listed = self.table[base + self.block_count + block * self.list_cap + entry]
+        return block, jnp.where(live, listed, 0), live
+
+    def sides(self):
+        for side in range(2):
+            for s in range(self.slots):
+                yield (side * self.slots + s, side, s) + self.slot(side, s)
+
+
+def own_scores_kernel(local, queries, _, keep, send):
+    rows = keep.shape[0]
+    core = lax.axis_index("grp") & 1
+    q = queries[...]
+    keep[...] = dot(local[pl.ds(core * rows, rows), :], q, NT)
+    send[...] = dot(local[pl.ds((1 - core) * rows, rows), :], q, NT)
+
+
+def listed_rows(pieces, listed):
+    rows, pieces = [], list(pieces)
+    total = pieces[0].shape[0]
+    while pieces:
+        first, row = 0, None
+        while first < total:
+            piece = pieces.pop(0)
+            part = piece[jnp.clip(listed - first, 0, piece.shape[0] - 1)]
+            row = part if row is None else jnp.where(listed >= first, part, row)
+            first += piece.shape[0]
+        rows.append(row)
+    return jnp.concatenate(rows, axis=0)
+
+
+def listed_scores_kernel(lists_of, table, queries, *refs):
+    sources, pieces, (keep, send, scores) = refs[:2], refs[2:-3], refs[-3:]
+    lists = lists_of(table)
+    slots, block_size = keep.shape[0], keep.shape[2]
+    core = lax.axis_index("grp") & 1
+    for place, side, _, block, listed, _ in lists.sides():
+        at = pl.ds(block * block_size, block_size)
+        rows = far_rows(sources, at) if side else queries[at, :]
+        scores[place] = dot(listed_rows(pieces, listed), rows, NT)
+    keep[...] = scores[pl.ds(core * slots, slots)]
+    send[...] = scores[pl.ds((1 - core) * slots, slots)]
+
+
+def lend_kernel(lists_of, first, table, *refs):
+    pieces, loan = refs[:-1], refs[-1]
+    lists = lists_of(table)
+    for i in range(loan.shape[0]):
+        _, listed, _ = lists.slot(1, first + i)
+        loan[i] = listed_rows(pieces, listed)
+
+
+def select_block(values, block):
+    picked = values[0]
+    for b in range(1, len(values)):
+        picked = jnp.where(block == b, values[b], picked)
+    return picked
+
+
+def cut(row, size):
+    return [row[:, i : i + size] for i in range(0, row.shape[1], size)]
+
+
+def stats_kernel(
+    lists_of, scale, table, in_half, in_other, list_half, list_other, per_query,
+    scores_in, scores_list, stats,
+):
+    lists = lists_of(table)
+    core = lax.axis_index("grp") & 1
+    rows, slots, block_size = in_half.shape[0], lists.slots, list_half.shape[2]
+    scores_in[pl.ds(core * rows, rows), :] = scale * in_half[...]
+    scores_in[pl.ds((1 - core) * rows, rows), :] = scale * in_other[...]
+    scores_list[pl.ds(core * slots, slots)] = scale * list_half[...]
+    scores_list[pl.ds((1 - core) * slots, slots)] = scale * list_other[...]
+    near = scores_in[...]
+    info = list(lists.sides())
+    for side in range(2):
+        listed = [entry for entry in info if entry[1] == side]
+        scores = [scores_list[entry[0]] for entry in listed]
+        if side:
+            peaks = [jnp.full((1, block_size), -jnp.inf, jnp.float32)] * lists.block_count
+        else:
+            peaks = cut(jnp.max(near, axis=0, keepdims=True), block_size)
+        for entry, score in zip(listed, scores):
+            slot_peak = jnp.max(score, axis=0, keepdims=True)
+            for b in range(lists.block_count):
+                counts = (entry[3] == b) & entry[5]
+                peaks[b] = jnp.maximum(peaks[b], jnp.where(counts, slot_peak, -jnp.inf))
+        row_peak = jnp.concatenate(peaks, axis=1)
+        if side:
+            totals = [jnp.zeros((1, block_size), jnp.float32)] * lists.block_count
+        else:
+            totals = cut(jnp.sum(jnp.exp(near - row_peak), axis=0, keepdims=True), block_size)
+        for entry, score in zip(listed, scores):
+            shifted = jnp.exp(score - select_block(peaks, entry[3]))
+            slot_sum = jnp.sum(shifted, axis=0, keepdims=True)
+            for b in range(lists.block_count):
+                counts = (entry[3] == b) & entry[5]
+                totals[b] = totals[b] + jnp.where(counts, slot_sum, 0.0)
+        stats[2 * side : 2 * side + 1, :] = row_peak
+        stats[2 * side + 1 : 2 * side + 2, :] = jnp.concatenate(totals, axis=1)
+    stats[4:5, :] = per_query[0:1, :]
+    stats[5:8, :] = jnp.zeros((3, stats.shape[1]), jnp.float32)
+
+
+def log_sum(near, far):
+    peak = jnp.maximum(near[0], far[0])
+    return peak + jnp.log(near[1] * jnp.exp(near[0] - peak) + far[1] * jnp.exp(far[0] - peak))
+
+
+def weights_kernel(
+    lists_of, scale, table, scores_in, scores_list, stats, far_stats, per_query, queries,
+    near_source, far_source, losses, weights_in, weights_own, weights_loan, *shares,
+):
+    lists = lists_of(table)
+    block_size = scores_list.shape[2]
+    shard_rows = shares[0].shape[1]
+    rows = [stats[i : i + 1, :] for i in range(5)]
+    mirrored = [far_stats[i : i + 1, :] for i in range(5)]
+    log_total = log_sum(rows[0:2], mirrored[2:4])
+    far_log = log_sum(mirrored[0:2], rows[2:4])
+    grad = rows[4]
+    logs = cut(log_total, block_size), cut(far_log, block_size)
+    grads = cut(grad, block_size), cut(mirrored[4], block_size)
+    for place, side, s, block, _, live in lists.sides():
+        weight = jnp.where(
+            live,
+            select_block(grads[side], block)
+            * jnp.exp(scores_list[place] - select_block(logs[side], block)),
+            0.0,
+        ).astype(jnp.bfloat16)
+        (weights_loan if side else weights_own)[s] = weight
+        at = pl.ds(block * block_size, block_size)
+        share = scale * dot(weight, far_rows((near_source, far_source), at) if side else queries[at, :])
+        share = share.astype(jnp.bfloat16)
+        for k, out in enumerate(shares):
+            out[place] = share[k * shard_rows : (k + 1) * shard_rows]
+    near = scores_in[...]
+    pos_column = per_query[1:2, :].astype(jnp.int32)
+    is_positive = lax.broadcasted_iota(jnp.int32, near.shape, 0) == pos_column
+    positive_score = jnp.sum(jnp.where(is_positive, near, 0.0), axis=0, keepdims=True)
+    losses[...] = log_total - positive_score
+    weights_in[...] = (
+        grad * (jnp.exp(near - log_total) - is_positive.astype(jnp.float32))
+    ).astype(jnp.bfloat16)
+
+
+def own_grads_kernel(
+    lists_of, scale, table, weights_in, weights_own, queries, local, own_share, *refs
+):
+    pieces, (query_total, own_part) = refs[:-2], refs[-2:]
+    lists = lists_of(table)
+    block_size, shard_rows = weights_own.shape[2], own_share.shape[1]
+    near = weights_in[...]
+    query_total[...] = dot(near, local[...], TN)
+    own_part[...] = scale * dot(near, queries[...])
+    for place, side, s, block, listed, _ in lists.sides():
+        if not side:
+            rows = listed_rows(pieces, listed)
+            at = pl.ds(block * block_size, block_size)
+            query_total[at, :] = query_total[at, :] + dot(weights_own[s], rows, TN)
+        at = pl.ds(listed * shard_rows, shard_rows)
+        own_part[at, :] = own_part[at, :] + own_share[place].astype(jnp.float32)
+
+
+def far_grads_kernel(lists_of, scale, table, query_total, weights_far, *refs):
+    loans, (grad_queries, total) = refs[:-2], refs[-2:]
+    borrowed = [loan.at[i] for loan in loans for i in range(loan.shape[0])]
+    lists = lists_of(table)
+    block_size = weights_far.shape[2]
+    total[...] = query_total[...]
+    for _, side, s, block, _, _ in lists.sides():
+        if not side:
+            at = pl.ds(block * block_size, block_size)
+            total[at, :] = total[at, :] + dot(weights_far[s], borrowed[s][...], TN)
+    grad_queries[...] = (scale * total[...]).astype(jnp.bfloat16)
+
+
+def collect_kernel(lists_of, own_part, *refs):
+    (*inputs, grad_passages, total), count = refs, (len(refs) - 2) // 2
+    tables, returned = inputs[:count], inputs[count:]
+    shard_rows = returned[0].shape[1]
+    total[...] = own_part[...]
+    for table, piece in zip(tables, returned):
+        for place, _, _, _, listed, _ in lists_of(table).sides():
+            at = pl.ds(listed * shard_rows, shard_rows)
+            total[at, :] = total[at, :] + piece[place].astype(jnp.float32)
+    grad_passages[...] = total[...].astype(jnp.bfloat16)
+
+
+def local_call(kernel, outs, scratch=(), hbm=()):
+    shapes = [
+        jax.ShapeDtypeStruct(*out) if i in hbm or out[1] == jnp.int32 else pltpu.VMEM(*out)
+        for i, out in enumerate(outs)
+    ]
+    smem, vmem = (pl.BlockSpec(memory_space=space) for space in (pltpu.SMEM, pltpu.VMEM))
+
+    def call(*args):
+        tables = [arg.dtype == jnp.int32 for arg in args]
+        placed = [
+            arg if table else pltpu.with_memory_space_constraint(arg, pltpu.VMEM)
+            for arg, table in zip(args, tables)
+        ]
+        return pl.pallas_call(
+            kernel,
+            out_shape=shapes,
+            in_specs=[smem if table else vmem for table in tables],
+            out_specs=[smem if out[1] == jnp.int32 else vmem for out in outs],
+            scratch_shapes=[pltpu.VMEM(shape, dtype) for shape, dtype in scratch],
+            compiler_params=pltpu.CompilerParams(vmem_limit_bytes=KERNEL_VMEM),
+        )(*placed)
+
+    return call
+
+
+def mirror_plan(queries, passages, block_lists, list_lengths, positive, loss_grad):
+    bf16, f32 = jnp.bfloat16, jnp.float32
+    scale = 3.0 / math.sqrt(D)
+    dp_count, me = lax.axis_size("dp"), lax.axis_index("dp")
+    block_count, list_cap = block_lists.shape
+    block_total, shard_rows, width = passages.shape
+    block_size = shard_rows * dp_count
+    query_rows = queries.shape[0]
+    own_rows = block_total * shard_rows
+    slots = LIVE_MAX
+    half = dp_count // 2
+    flip = half | half >> 1
+    half_rows = half * shard_rows
+    peers = range(1, half)
+    lists_of = functools.partial(
+        Lists, block_count=block_count, list_cap=list_cap, slots=slots
+    )
+
+    cut_at = block_total * 3 // 4
+    chunks = [passages[:cut_at], passages[cut_at:]]
+    by_peer = {0: [passages]}
+    for k in sorted(peers, key=lambda k: (k.bit_count(), -k)):
+        low = k & -k
+        if k == 1:
+            by_peer[k] = [swap(passages, "dp", low)]
+        elif k == low:
+            by_peer[k] = [swap(chunk, "dp", low) for chunk in chunks]
+        else:
+            by_peer[k] = [swap(chunk, "dp", low) for chunk in by_peer[k ^ low]]
+    pieces = [chunk for k in range(half) for chunk in by_peer[k]]
+    far_queries = (
+        swap(queries, "dp", flip, inner), swap(queries, "dp", flip, lambda i: not inner(i))
+    )
+    mine = jnp.concatenate([list_lengths, block_lists.reshape(-1)])
+    far_mine = swap(mine, "dp", flip)
+    (table,) = local_call(join_kernel, [((2 * mine.shape[0],), jnp.int32)])(mine, far_mine)
+    tables = [swap(table, "dp", k) for k in peers]
+    pos_column = positive // block_size * shard_rows + positive % block_size - me * shard_rows
+    per_query = jnp.stack([loss_grad, pos_column.astype(f32)])
+
+    local = passages.reshape(own_rows, width)
+    in_half = ((own_rows // 2, query_rows), f32)
+    keep_in, send_in = local_call(own_scores_kernel, [in_half, in_half])(local, queries, per_query)
+    in_sums = sum_over_grp(keep_in, send_in)
+
+    list_half = ((slots, half_rows, block_size), f32)
+    keep_list, send_list = local_call(
+        functools.partial(listed_scores_kernel, lists_of),
+        [list_half, list_half],
+        scratch=[((2 * slots, half_rows, block_size), f32)],
+    )(table, queries, *far_queries, *pieces)
+
+    borrowed = []
+    for i, count in enumerate(LOANS):
+        (loan,) = local_call(
+            functools.partial(lend_kernel, lists_of, sum(LOANS[:i])),
+            [((count, half_rows, width), bf16)],
+        )(table, *pieces)
+        borrowed.append(swap(loan, "dp", flip))
+    list_sums = sum_over_grp(keep_list, send_list)
+
+    scores_in, scores_list, stats = local_call(
+        functools.partial(stats_kernel, lists_of, scale),
+        [
+            ((own_rows, query_rows), f32),
+            ((2 * slots, half_rows, block_size), f32),
+            ((8, query_rows), f32),
+        ],
+    )(table, *in_sums, *list_sums, per_query)
+    far_stats = swap_shared(stats, flip)
+
+    weights_half = ((slots, half_rows, block_size), bf16)
+    piece = ((2 * slots, shard_rows, width), bf16)
+    losses, weights_in, weights_own, weights_loan, *shares = local_call(
+        functools.partial(weights_kernel, lists_of, scale),
+        [((1, query_rows), f32), ((own_rows, query_rows), bf16), weights_half, weights_half]
+        + [piece] * half,
+        hbm=(0,),
+    )(table, scores_in, scores_list, stats, far_stats, per_query, queries, *far_queries)
+    returned = [swap(shares[k], "dp", k) for k in reversed(peers)][::-1]
+    weights_far = swap_shared(weights_loan, flip)
+
+    query_total, own_part = local_call(
+        functools.partial(own_grads_kernel, lists_of, scale),
+        [((query_rows, width), f32), ((own_rows, width), f32)],
+    )(table, weights_in, weights_own, queries, local, shares[0], *pieces)
+    (grad_queries,) = local_call(
+        functools.partial(far_grads_kernel, lists_of, scale),
+        [((query_rows, width), bf16)],
+        scratch=[((query_rows, width), f32)],
+        hbm=(0,),
+    )(table, query_total, weights_far, *borrowed)
+    (grad_passages,) = local_call(
+        functools.partial(collect_kernel, lists_of),
+        [((own_rows, width), bf16)],
+        scratch=[((own_rows, width), f32)],
+        hbm=(0,),
+    )(own_part, *tables, *returned)
+    return (
+        losses.reshape(query_rows),
+        grad_queries,
+        grad_passages.reshape(block_total, shard_rows, width),
+    )
+
+
+def per_device(queries, passages, block_lists, list_lengths, positive, loss_grad):
+    plan = mirror_plan if mirror_fits(passages.shape) else exchange_plan
+    return plan(queries, passages, block_lists, list_lengths, positive, loss_grad)
+
+
 def solution(mesh):
     in_specs = (P("dp", "grp"), P(None, "dp", "grp"), P("dp", None), P("dp"), P("dp"), P("dp"))
     out_specs = (P("dp"), P("dp", "grp"), P(None, "dp", "grp"))

time: 146 us -> 101 us (0.69)
  starting transfers between devices: 9.11 us -> 37.9 us
  waiting for transfers between devices: 71.5 us -> 46.4 us
  between operations: 14.9 us -> 0.81 us
  other arithmetic: 14.1 us -> 0.75 us
  blocking collectives: 13.1 us -> 0 us
  Pallas kernels: 0 us -> 12 us
  matrix products: 11.5 us -> 0 us
  local copies, waits for them, and re-layouts: 11.5 us -> 3.22 us
    ppermute x0 -> x25, waiting for transfers between devices: none -> 46.4 us  [the longest x23 43.3 us: swap(): return lax.ppermute(value, axis, pairs)]
    all_to_all x2 -> x0, waiting for transfers between devices: 39 us -> none  [the longest x1 20.2 us: per_device(): lax.all_to_all(outgoing, 'dp', split_axis=0, concat_axis=2, tiled=True)]
    ppermute x0 -> x25, starting transfers between devices: none -> 37.9 us  [the longest x23 35.2 us: swap(): return lax.ppermute(value, axis, pairs)]
    psum x1 -> x0, waiting for transfers between devices: 32.5 us -> none  [per_device(): full_in, full_list = lax.psum((part_in, part_list), 'grp')]
    unnamed x1 -> x0, blocking collectives: 13.1 us -> none
    pallas_call x0 -> x15, Pallas kernels: none -> 12 us  [call(): pl.pallas_call(kernel, out_shape=shapes, in_specs=[smem if table else vme...]
    dot_general x8 -> x0, matrix products: 11.5 us -> none  [the longest x1 3.25 us: per_device(): jnp.einsum('sb,sqf->bqf', block_match.astype(jnp.float32), per_slot, prec...]
    all_to_all x2 -> x0, starting transfers between devices: 9.07 us -> none  [the longest x1 5.51 us: per_device(): lax.all_to_all(shares.reshape(1, slot_count, block_size, feature_width),...]
  transfers between devices with their start and end apart: 3 -> 25, of which waited for: 3 -> 9; matrix products, arithmetic and copies ran while one was open for 6% -> 2% of each run, Pallas kernels for 0% -> 10%
where the time goes in v1:
time: 101 us
  waiting for transfers between devices  46.4 us (46%)
  starting transfers between devices  37.9 us (38%)
  Pallas kernels  12 us (12%)
  local copies, waits for them, and re-layouts  3.22 us (3%)
    ppermute x23, waiting for transfers between devices, swap(): return lax.ppermute(value, axis, pairs)  43.3 us
    ppermute x23, starting transfers between devices, swap(): return lax.ppermute(value, axis, pairs)  35.2 us
    pallas_call x15, Pallas kernels, call(): pl.pallas_call(kernel, out_shape=shapes, in_specs=[smem if table else vme...  12 us
    ppermute x2, waiting for transfers between devices, swap_shared(): return lax.ppermute(value, ('dp', 'grp'), pairs)  3.1 us
    ppermute x2, starting transfers between devices, swap_shared(): return lax.ppermute(value, ('dp', 'grp'), pairs)  2.7 us
  transfers between devices with their start and end apart: 25, of which 9 were waited for; matrix products, arithmetic and copies ran while one was open for 2% of the time, Pallas kernels for 10%

profile of v1, /device:TPU:0, one launch (start us, length us, event | category | flops | bytes accessed | tf_op | source)
XLA Modules:
  0.0 101.0 jit_solution(7266038746174401989)
XLA Ops:
  1.8 3.1 %collective-permute-start.7 = (bf16[12,16,1024]{2,1,0:T(8,128)(2,1)S(1)}, bf16[12,16,1024]{2,1,0:T(8,128)(2,1)S(1)}, u32[]{:S(2)}, u32[]{:S(2)}) collective-permute-start(bf16[12,16,1024]{2,1,0:T(8,128)(2,1)S(1)} %slice.6), channel_id=1, source_target_pairs={{0,8},{4,12},{8,0},{12,4},{16,24},{20,28},{24,16},{28,20},{1,9},{5... | collective-permute-start | bytes 1179656 | tf_op jit(solution)/shard_map/ppermute | solution.py:153
  4.9 1.5 %collective-permute-start.6 = (bf16[16,16,1024]{2,1,0:T(8,128)(2,1)S(1)}, bf16[16,16,1024]{2,1,0:T(8,128)(2,1)S(1)}, u32[]{:S(2)}, u32[]{:S(2)}) collective-permute-start(bf16[16,16,1024]{2,1,0:T(8,128)(2,1)S(1)} %copy-done), channel_id=1, source_target_pairs={{0,4},{4,0},{8,12},{12,8},{16,20},{20,16},{24,28},{28,24},{1,5},{5... | collective-permute-start | bytes 1572872 | tf_op jit(solution)/shard_map/ppermute | solution.py:153
  7.1 4.4 %collective-permute-start.5 = (bf16[256,1024]{1,0:T(8,128)(2,1)}, bf16[256,1024]{1,0:T(8,128)(2,1)S(1)}, u32[]{:S(2)}, u32[]{:S(2)}) collective-permute-start(bf16[256,1024]{1,0:T(8,128)(2,1)} %queries.7), channel_id=1, source_target_pairs={{0,24},{4,28},{24,0},{28,4},{1,25},{5,29},{25,1},{29,5},{2,26},{6,... | collective-permute-start | bytes 1572872 | tf_op jit(solution)/shard_map/ppermute | solution.py:153
  13.0 1.3 %collective-permute-start = (s32[8]{0:T(128)S(1)}, s32[8]{0:T(128)S(1)}, u32[]{:S(2)}, u32[]{:S(2)}) collective-permute-start(s32[8]{0:T(128)S(1)} %pad_add_fusion.a), channel_id=1, source_target_pairs={{0,24},{4,28},{8,16},{12,20},{16,8},{20,12},{24,0},{28,4},{1,25},{... | collective-permute-start | bytes 104 | tf_op jit(solution)/shard_map/ppermute | solution.py:153
  15.0 12.7 %collective-permute-done.b = s32[8]{0:T(128)S(1)} collective-permute-done((s32[8]{0:T(128)S(1)}, s32[8]{0:T(128)S(1)}, u32[]{:S(2)}, u32[]{:S(2)}) %collective-permute-start) | collective-permute-done | bytes 64 | tf_op jit(solution)/shard_map/ppermute | solution.py:153
  27.6 6.7 %collective-permute-start.8 = (bf16[4,16,1024]{2,1,0:T(8,128)(2,1)}, bf16[4,16,1024]{2,1,0:T(8,128)(2,1)S(1)}, u32[]{:S(2)}, u32[]{:S(2)}) collective-permute-start(bf16[4,16,1024]{2,1,0:T(8,128)(2,1)} %slice.7), channel_id=1, source_target_pairs={{0,8},{4,12},{8,0},{12,4},{16,24},{20,28},{24,16},{28,20},{1,9},{5... | collective-permute-start | bytes 393224 | tf_op jit(solution)/shard_map/ppermute | solution.py:153
  34.9 2.6 %collective-permute-done.8.refs_5_.refs_3_ = bf16[4,16,1024]{2,1,0:T(8,128)(2,1)S(1)} collective-permute-done((bf16[4,16,1024]{2,1,0:T(8,128)(2,1)}, bf16[4,16,1024]{2,1,0:T(8,128)(2,1)S(1)}, u32[]{:S(2)}, u32[]{:S(2)}) %collective-permute-start.8) | collective-permute-done | bytes 131104 | tf_op jit(solution)/shard_map/ppermute | solution.py:153
  40.4 6.1 %collective-permute-done.10.refs_7_.refs_5_ = bf16[4,16,1024]{2,1,0:T(8,128)(2,1)S(1)} collective-permute-done((bf16[4,16,1024]{2,1,0:T(8,128)(2,1)S(1)}, bf16[4,16,1024]{2,1,0:T(8,128)(2,1)S(1)}, u32[]{:S(2)}, u32[]{:S(2)}) %collective-permute-start.10) | collective-permute-done | bytes 131104 | tf_op jit(solution)/shard_map/ppermute | solution.py:153
  46.5 1.4 %shard_map.89 = (f32[4,64,128]{2,1,0:T(8,128)S(1)}, f32[4,64,128]{2,1,0:T(8,128)S(1)}) custom-call(s32[16]{0:T(128)S(1)} %shard_map.85.table, bf16[256,1024]{1,0:T(8,128)(2,1)S(1)} %copy-done.1, bf16[256,1024]{1,0:T(8,128)(2,1)S(1)} %collective-permute-done.4.refs_0_.near_source, bf16[256,1024]{1,0:T(8,128)(2,1)S(1)} %collective-permute-done.5.refs_1_.far_source, ...), custom_call_target="tpu_custom_call" | custom-call | tf_op jit(solution)/shard_map/pallas_call | solution.py:422
  48.6 1.6 %collective-permute-start.2 = (f32[128,256]{1,0:T(8,128)S(1)}, f32[128,256]{1,0:T(8,128)S(1)}, u32[]{:S(2)}, u32[]{:S(2)}) collective-permute-start(f32[128,256]{1,0:T(8,128)S(1)} %shard_map.87.a), channel_id=1, source_target_pairs={{0,2},{1,3},{2,0},{3,1},{4,6},{5,7},{6,4},{7,5},{8,10},{9,11},{10,... | collective-permute-start | bytes 393224 | tf_op jit(solution)/shard_map/ppermute | solution.py:153
  51.1 3.9 %collective-permute-done.2.b = f32[128,256]{1,0:T(8,128)S(1)} collective-permute-done((f32[128,256]{1,0:T(8,128)S(1)}, f32[128,256]{1,0:T(8,128)S(1)}, u32[]{:S(2)}, u32[]{:S(2)}) %collective-permute-start.2) | collective-permute-done | bytes 131104 | tf_op jit(solution)/shard_map/ppermute | solution.py:153
  55.1 1.8 %collective-permute-done.12.b = f32[4,64,128]{2,1,0:T(8,128)S(1)} collective-permute-done((f32[4,64,128]{2,1,0:T(8,128)S(1)}, f32[4,64,128]{2,1,0:T(8,128)S(1)}, u32[]{:S(2)}, u32[]{:S(2)}) %collective-permute-start.12) | collective-permute-done | bytes 131104 | tf_op jit(solution)/shard_map/ppermute | solution.py:153
  57.6 2.4 %collective-permute-start.17 = (bf16[1,64,1024]{2,1,0:T(8,128)(2,1)S(1)}, bf16[1,64,1024]{2,1,0:T(8,128)(2,1)S(1)}, u32[]{:S(2)}, u32[]{:S(2)}) collective-permute-start(bf16[1,64,1024]{2,1,0:T(8,128)(2,1)S(1)} %shard_map.96), channel_id=1, source_target_pairs={{0,24},{4,28},{8,16},{12,20},{16,8},{20,12},{24,0},{28,4},{1,25},{... | collective-permute-start | bytes 393224 | tf_op jit(solution)/shard_map/ppermute | solution.py:153
  60.7 1.4 %collective-permute-start.14 = (f32[8,256]{1,0:T(8,128)S(1)}, f32[8,256]{1,0:T(8,128)S(1)}, u32[]{:S(2)}, u32[]{:S(2)}) collective-permute-start(f32[8,256]{1,0:T(8,128)S(1)} %get-tuple-element.26.stats), channel_id=1, source_target_pairs={{0,25},{1,24},{2,27},{3,26},{4,29},{5,28},{6,31},{7,30},{8,17},{9,... | collective-permute-start | bytes 24584 | tf_op jit(solution)/shard_map/ppermute | solution.py:173
  62.6 2.4 %collective-permute-start.16 = (bf16[2,64,1024]{2,1,0:T(8,128)(2,1)S(1)}, bf16[2,64,1024]{2,1,0:T(8,128)(2,1)S(1)}, u32[]{:S(2)}, u32[]{:S(2)}) collective-permute-start(bf16[2,64,1024]{2,1,0:T(8,128)(2,1)S(1)} %shard_map.95), channel_id=1, source_target_pairs={{0,24},{4,28},{8,16},{12,20},{16,8},{20,12},{24,0},{28,4},{1,25},{... | collective-permute-start | bytes 786440 | tf_op jit(solution)/shard_map/ppermute | solution.py:153
  65.6 1.6 %shard_map.93 = (f32[1,256]{1,0:T(1,128)}, bf16[256,256]{1,0:T(8,128)(2,1)S(1)}, bf16[4,64,128]{2,1,0:T(8,128)(2,1)S(1)}, bf16[4,64,128]{2,1,0:T(8,128)(2,1)S(1)...) custom-call(s32[16]{0:T(128)S(1)} %shard_map.85.table, ...), custom_call_target="tpu_custom_call" | custom-call | tf_op jit(solution)/shard_map/pallas_call | solution.py:422
  68.5 2.2 %collective-permute-start.24 = (bf16[8,16,1024]{2,1,0:T(8,128)(2,1)S(1)}, bf16[8,16,1024]{2,1,0:T(8,128)(2,1)S(1)}, u32[]{:S(2)}, u32[]{:S(2)}) collective-permute-start(bf16[8,16,1024]{2,1,0:T(8,128)(2,1)S(1)} %get-tuple-element.36), channel_id=1, source_target_pairs={{0,12},{4,8},{8,4},{12,0},{16,28},{20,24},{24,20},{28,16},{1,13},{... | collective-permute-start | bytes 786440 | tf_op jit(solution)/shard_map/ppermute | solution.py:153
  71.3 1.9 %collective-permute-start.18 = (bf16[1,64,1024]{2,1,0:T(8,128)(2,1)S(1)}, bf16[1,64,1024]{2,1,0:T(8,128)(2,1)S(1)}, u32[]{:S(2)}, u32[]{:S(2)}) collective-permute-start(bf16[1,64,1024]{2,1,0:T(8,128)(2,1)S(1)} %shard_map.97), channel_id=1, source_target_pairs={{0,24},{4,28},{8,16},{12,20},{16,8},{20,12},{24,0},{28,4},{1,25},{... | collective-permute-start | bytes 393224 | tf_op jit(solution)/shard_map/ppermute | solution.py:153
  73.2 14.0 %collective-permute-done.18.refs_2_ = bf16[1,64,1024]{2,1,0:T(8,128)(2,1)S(1)} collective-permute-done((bf16[1,64,1024]{2,1,0:T(8,128)(2,1)S(1)}, bf16[1,64,1024]{2,1,0:T(8,128)(2,1)S(1)}, u32[]{:S(2)}, u32[]{:S(2)}) %collective-permute-start.18) | collective-permute-done | bytes 131104 | tf_op jit(solution)/shard_map/ppermute | solution.py:153
  90.5 2.5 %collective-permute-done.15.weights_far = bf16[4,64,128]{2,1,0:T(8,128)(2,1)S(1)} collective-permute-done((bf16[4,64,128]{2,1,0:T(8,128)(2,1)S(1)}, bf16[4,64,128]{2,1,0:T(8,128)(2,1)S(1)}, u32[]{:S(2)}, u32[]{:S(2)}) %collective-permute-start.15) | collective-permute-done | bytes 65568 | tf_op jit(solution)/shard_map/ppermute | solution.py:173
  93.0 1.9 %shard_map.98 = bf16[256,1024]{1,0:T(8,128)(2,1)} custom-call(s32[16]{0:T(128)S(1)} %shard_map.85.table, f32[256,1024]{1,0:T(8,128)S(1)} %get-tuple-element.31.query_total, bf16[4,64,128]{2,1,0:T(8,128)(2,1)S(1)} %collective-permute-done.15.weights_far, bf16[2,64,1024]{2,1,0:T(8,128)(2,1)S(1)} %collective-permute-done.16.refs_0_, ...), custom_call_target="tpu_custom_call" | custom-call | tf_op jit(solution)/shard_map/pallas_call | solution.py:422
  94.9 2.3 %collective-permute-start.21 = (s32[16]{0:T(128)S(1)}, s32[16]{0:T(128)S(1)}, u32[]{:S(2)}, u32[]{:S(2)}) collective-permute-start(s32[16]{0:T(128)S(1)} %shard_map.85.table), channel_id=1, source_target_pairs={{0,12},{4,8},{8,4},{12,0},{16,28},{20,24},{24,20},{28,16},{1,13},{... | collective-permute-start | bytes 200 | tf_op jit(solution)/shard_map/ppermute | solution.py:153
  97.2 2.1 %collective-permute-done.21.refs_2_ = s32[16]{0:T(128)S(1)} collective-permute-done((s32[16]{0:T(128)S(1)}, s32[16]{0:T(128)S(1)}, u32[]{:S(2)}, u32[]{:S(2)}) %collective-permute-start.21) | collective-permute-done | bytes 96 | tf_op jit(solution)/shard_map/ppermute | solution.py:153
  99.4 1.7 %shard_map.99 = bf16[256,1024]{1,0:T(8,128)(2,1)} custom-call(f32[256,1024]{1,0:T(8,128)S(1)} %get-tuple-element.33.own_part, s32[16]{0:T(128)S(1)} %collective-permute-done.19.refs_0_, s32[16]{0:T(128)S(1)} %collective-permute-done.20.refs_1_, s32[16]{0:T(128)S(1)} %collective-permute-done.21.refs_2_, ...), custom_call_target="tpu_custom_call" | custom-call | tf_op jit(solution)/shard_map/pallas_call | solution.py:422
  (55 shorter events, 16.7 us)
Async XLA Ops:
  1.8 32.6 %collective-permute-start.7 = (bf16[12,16,1024]{2,1,0:T(8,128)(2,1)S(1)}, bf16[12,16,1024]{2,1,0:T(8,128)(2,1)S(1)}, u32[]{:S(2)}, u32[]{:S(2)}) collective-permute-start(bf16[12,16,1024]{2,1,0:T(8,128)(2,1)S(1)} %slice.6), channel_id=1, source_target_pairs={{0,8},{4,12},{8,0},{12,4},{16,24},{20,28},{24,16},{28,20},{1,9},{5... | collective-permute-start | bytes 1179656 | tf_op jit(solution)/shard_map/ppermute | solution.py:153
  4.9 41.6 %collective-permute-start.6 = (bf16[16,16,1024]{2,1,0:T(8,128)(2,1)S(1)}, bf16[16,16,1024]{2,1,0:T(8,128)(2,1)S(1)}, u32[]{:S(2)}, u32[]{:S(2)}) collective-permute-start(bf16[16,16,1024]{2,1,0:T(8,128)(2,1)S(1)} %copy-done), channel_id=1, source_target_pairs={{0,4},{4,0},{8,12},{12,8},{16,20},{20,16},{24,28},{28,24},{1,5},{5... | collective-permute-start | bytes 1572872 | tf_op jit(solution)/shard_map/ppermute | solution.py:153
  6.4 40.1 %collective-permute-start.4 = (bf16[256,1024]{1,0:T(8,128)(2,1)}, bf16[256,1024]{1,0:T(8,128)(2,1)S(1)}, u32[]{:S(2)}, u32[]{:S(2)}) collective-permute-start(bf16[256,1024]{1,0:T(8,128)(2,1)} %queries.7), channel_id=1, source_target_pairs={{8,16},{12,20},{16,8},{20,12},{9,17},{13,21},{17,9},{21,13},{10,18... | collective-permute-start | bytes 1572872 | tf_op jit(solution)/shard_map/ppermute | solution.py:153
  7.1 39.5 %collective-permute-start.5 = (bf16[256,1024]{1,0:T(8,128)(2,1)}, bf16[256,1024]{1,0:T(8,128)(2,1)S(1)}, u32[]{:S(2)}, u32[]{:S(2)}) collective-permute-start(bf16[256,1024]{1,0:T(8,128)(2,1)} %queries.7), channel_id=1, source_target_pairs={{0,24},{4,28},{24,0},{28,4},{1,25},{5,29},{25,1},{29,5},{2,26},{6,... | collective-permute-start | bytes 1572872 | tf_op jit(solution)/shard_map/ppermute | solution.py:153
  13.0 14.7 %collective-permute-start = (s32[8]{0:T(128)S(1)}, s32[8]{0:T(128)S(1)}, u32[]{:S(2)}, u32[]{:S(2)}) collective-permute-start(s32[8]{0:T(128)S(1)} %pad_add_fusion.a), channel_id=1, source_target_pairs={{0,24},{4,28},{8,16},{12,20},{16,8},{20,12},{24,0},{28,4},{1,25},{... | collective-permute-start | bytes 104 | tf_op jit(solution)/shard_map/ppermute | solution.py:153
  27.6 9.9 %collective-permute-start.8 = (bf16[4,16,1024]{2,1,0:T(8,128)(2,1)}, bf16[4,16,1024]{2,1,0:T(8,128)(2,1)S(1)}, u32[]{:S(2)}, u32[]{:S(2)}) collective-permute-start(bf16[4,16,1024]{2,1,0:T(8,128)(2,1)} %slice.7), channel_id=1, source_target_pairs={{0,8},{4,12},{8,0},{12,4},{16,24},{20,28},{24,16},{28,20},{1,9},{5... | collective-permute-start | bytes 393224 | tf_op jit(solution)/shard_map/ppermute | solution.py:153
  34.3 12.2 %collective-permute-start.9 = (bf16[12,16,1024]{2,1,0:T(8,128)(2,1)S(1)}, bf16[12,16,1024]{2,1,0:T(8,128)(2,1)S(1)}, u32[]{:S(2)}, u32[]{:S(2)}) collective-permute-start(bf16[12,16,1024]{2,1,0:T(8,128)(2,1)S(1)} %collective-permute-done.7.refs_4_.refs_2_), channel_id=1, source_target_pairs={{0,4},{4,0},{8,12},{12,8},{16,20},{20,16},{24,28},{28,24},{1,5},{5... | collective-permute-start | bytes 1179656 | tf_op jit(solution)/shard_map/ppermute | solution.py:153
  37.5 9.0 %collective-permute-start.10 = (bf16[4,16,1024]{2,1,0:T(8,128)(2,1)S(1)}, bf16[4,16,1024]{2,1,0:T(8,128)(2,1)S(1)}, u32[]{:S(2)}, u32[]{:S(2)}) collective-permute-start(bf16[4,16,1024]{2,1,0:T(8,128)(2,1)S(1)} %collective-permute-done.8.refs_5_.refs_3_), channel_id=1, source_target_pairs={{0,4},{4,0},{8,12},{12,8},{16,20},{20,16},{24,28},{28,24},{1,5},{5... | collective-permute-start | bytes 393224 | tf_op jit(solution)/shard_map/ppermute | solution.py:153
  48.0 2.2 %collective-permute-start.11 = (f32[4,64,128]{2,1,0:T(8,128)S(1)}, f32[4,64,128]{2,1,0:T(8,128)S(1)}, u32[]{:S(2)}, u32[]{:S(2)}) collective-permute-start(f32[4,64,128]{2,1,0:T(8,128)S(1)} %get-tuple-element.23), channel_id=1, source_target_pairs={{0,1},{1,0},{2,3},{3,2},{4,5},{5,4},{6,7},{7,6},{8,9},{9,8},{10,11... | collective-permute-start | bytes 393224 | tf_op jit(solution)/shard_map/ppermute | solution.py:153
  48.6 6.4 %collective-permute-start.2 = (f32[128,256]{1,0:T(8,128)S(1)}, f32[128,256]{1,0:T(8,128)S(1)}, u32[]{:S(2)}, u32[]{:S(2)}) collective-permute-start(f32[128,256]{1,0:T(8,128)S(1)} %shard_map.87.a), channel_id=1, source_target_pairs={{0,2},{1,3},{2,0},{3,1},{4,6},{5,7},{6,4},{7,5},{8,10},{9,11},{10,... | collective-permute-start | bytes 393224 | tf_op jit(solution)/shard_map/ppermute | solution.py:153
  50.2 6.7 %collective-permute-start.12 = (f32[4,64,128]{2,1,0:T(8,128)S(1)}, f32[4,64,128]{2,1,0:T(8,128)S(1)}, u32[]{:S(2)}, u32[]{:S(2)}) collective-permute-start(f32[4,64,128]{2,1,0:T(8,128)S(1)} %shard_map.90.a), channel_id=1, source_target_pairs={{0,2},{1,3},{2,0},{3,1},{4,6},{5,7},{6,4},{7,5},{8,10},{9,11},{10,... | collective-permute-start | bytes 393224 | tf_op jit(solution)/shard_map/ppermute | solution.py:153
  55.0 4.9 %collective-permute-start.3 = (f32[128,256]{1,0:T(8,128)S(1)}, f32[128,256]{1,0:T(8,128)S(1)}, u32[]{:S(2)}, u32[]{:S(2)}) collective-permute-start(f32[128,256]{1,0:T(8,128)S(1)} %shard_map.88.in_half), channel_id=1, source_target_pairs={{0,1},{1,0},{2,3},{3,2},{4,5},{5,4},{6,7},{7,6},{8,9},{9,8},{10,11... | collective-permute-start | bytes 393224 | tf_op jit(solution)/shard_map/ppermute | solution.py:153
  56.9 3.1 %collective-permute-start.13 = (f32[4,64,128]{2,1,0:T(8,128)S(1)}, f32[4,64,128]{2,1,0:T(8,128)S(1)}, u32[]{:S(2)}, u32[]{:S(2)}) collective-permute-start(f32[4,64,128]{2,1,0:T(8,128)S(1)} %shard_map.91.list_half), channel_id=1, source_target_pairs={{0,1},{1,0},{2,3},{3,2},{4,5},{5,4},{6,7},{7,6},{8,9},{9,8},{10,11... | collective-permute-start | bytes 393224 | tf_op jit(solution)/shard_map/ppermute | solution.py:153
  57.6 13.7 %collective-permute-start.17 = (bf16[1,64,1024]{2,1,0:T(8,128)(2,1)S(1)}, bf16[1,64,1024]{2,1,0:T(8,128)(2,1)S(1)}, u32[]{:S(2)}, u32[]{:S(2)}) collective-permute-start(bf16[1,64,1024]{2,1,0:T(8,128)(2,1)S(1)} %shard_map.96), channel_id=1, source_target_pairs={{0,24},{4,28},{8,16},{12,20},{16,8},{20,12},{24,0},{28,4},{1,25},{... | collective-permute-start | bytes 393224 | tf_op jit(solution)/shard_map/ppermute | solution.py:153
  60.7 4.9 %collective-permute-start.14 = (f32[8,256]{1,0:T(8,128)S(1)}, f32[8,256]{1,0:T(8,128)S(1)}, u32[]{:S(2)}, u32[]{:S(2)}) collective-permute-start(f32[8,256]{1,0:T(8,128)S(1)} %get-tuple-element.26.stats), channel_id=1, source_target_pairs={{0,25},{1,24},{2,27},{3,26},{4,29},{5,28},{6,31},{7,30},{8,17},{9,... | collective-permute-start | bytes 24584 | tf_op jit(solution)/shard_map/ppermute | solution.py:173
  62.6 27.2 %collective-permute-start.16 = (bf16[2,64,1024]{2,1,0:T(8,128)(2,1)S(1)}, bf16[2,64,1024]{2,1,0:T(8,128)(2,1)S(1)}, u32[]{:S(2)}, u32[]{:S(2)}) collective-permute-start(bf16[2,64,1024]{2,1,0:T(8,128)(2,1)S(1)} %shard_map.95), channel_id=1, source_target_pairs={{0,24},{4,28},{8,16},{12,20},{16,8},{20,12},{24,0},{28,4},{1,25},{... | collective-permute-start | bytes 786440 | tf_op jit(solution)/shard_map/ppermute | solution.py:153
  67.2 32.1 %collective-permute-start.22 = (bf16[8,16,1024]{2,1,0:T(8,128)(2,1)S(1)}, bf16[8,16,1024]{2,1,0:T(8,128)(2,1)S(1)}, u32[]{:S(2)}, u32[]{:S(2)}) collective-permute-start(bf16[8,16,1024]{2,1,0:T(8,128)(2,1)S(1)} %get-tuple-element.34), channel_id=1, source_target_pairs={{0,4},{4,0},{8,12},{12,8},{16,20},{20,16},{24,28},{28,24},{1,5},{5... | collective-permute-start | bytes 786440 | tf_op jit(solution)/shard_map/ppermute | solution.py:153
  67.7 31.6 %collective-permute-start.23 = (bf16[8,16,1024]{2,1,0:T(8,128)(2,1)S(1)}, bf16[8,16,1024]{2,1,0:T(8,128)(2,1)S(1)}, u32[]{:S(2)}, u32[]{:S(2)}) collective-permute-start(bf16[8,16,1024]{2,1,0:T(8,128)(2,1)S(1)} %get-tuple-element.35), channel_id=1, source_target_pairs={{0,8},{4,12},{8,0},{12,4},{16,24},{20,28},{24,16},{28,20},{1,9},{5... | collective-permute-start | bytes 786440 | tf_op jit(solution)/shard_map/ppermute | solution.py:153
  68.5 30.9 %collective-permute-start.24 = (bf16[8,16,1024]{2,1,0:T(8,128)(2,1)S(1)}, bf16[8,16,1024]{2,1,0:T(8,128)(2,1)S(1)}, u32[]{:S(2)}, u32[]{:S(2)}) collective-permute-start(bf16[8,16,1024]{2,1,0:T(8,128)(2,1)S(1)} %get-tuple-element.36), channel_id=1, source_target_pairs={{0,12},{4,8},{8,4},{12,0},{16,28},{20,24},{24,20},{28,16},{1,13},{... | collective-permute-start | bytes 786440 | tf_op jit(solution)/shard_map/ppermute | solution.py:153
  71.3 15.9 %collective-permute-start.18 = (bf16[1,64,1024]{2,1,0:T(8,128)(2,1)S(1)}, bf16[1,64,1024]{2,1,0:T(8,128)(2,1)S(1)}, u32[]{:S(2)}, u32[]{:S(2)}) collective-permute-start(bf16[1,64,1024]{2,1,0:T(8,128)(2,1)S(1)} %shard_map.97), channel_id=1, source_target_pairs={{0,24},{4,28},{8,16},{12,20},{16,8},{20,12},{24,0},{28,4},{1,25},{... | collective-permute-start | bytes 393224 | tf_op jit(solution)/shard_map/ppermute | solution.py:153
  87.2 5.8 %collective-permute-start.15 = (bf16[4,64,128]{2,1,0:T(8,128)(2,1)S(1)}, bf16[4,64,128]{2,1,0:T(8,128)(2,1)S(1)}, u32[]{:S(2)}, u32[]{:S(2)}) collective-permute-start(bf16[4,64,128]{2,1,0:T(8,128)(2,1)S(1)} %get-tuple-element.32), channel_id=1, source_target_pairs={{0,25},{1,24},{2,27},{3,26},{4,29},{5,28},{6,31},{7,30},{8,17},{9,... | collective-permute-start | bytes 196616 | tf_op jit(solution)/shard_map/ppermute | solution.py:173
  89.9 5.0 %collective-permute-start.19 = (s32[16]{0:T(128)S(1)}, s32[16]{0:T(128)S(1)}, u32[]{:S(2)}, u32[]{:S(2)}) collective-permute-start(s32[16]{0:T(128)S(1)} %shard_map.85.table), channel_id=1, source_target_pairs={{0,4},{4,0},{8,12},{12,8},{16,20},{20,16},{24,28},{28,24},{1,5},{5... | collective-permute-start | bytes 200 | tf_op jit(solution)/shard_map/ppermute | solution.py:153
  93.0 4.2 %collective-permute-start.20 = (s32[16]{0:T(128)S(1)}, s32[16]{0:T(128)S(1)}, u32[]{:S(2)}, u32[]{:S(2)}) collective-permute-start(s32[16]{0:T(128)S(1)} %shard_map.85.table), channel_id=1, source_target_pairs={{0,8},{4,12},{8,0},{12,4},{16,24},{20,28},{24,16},{28,20},{1,9},{5... | collective-permute-start | bytes 200 | tf_op jit(solution)/shard_map/ppermute | solution.py:153
  94.9 4.5 %collective-permute-start.21 = (s32[16]{0:T(128)S(1)}, s32[16]{0:T(128)S(1)}, u32[]{:S(2)}, u32[]{:S(2)}) collective-permute-start(s32[16]{0:T(128)S(1)} %shard_map.85.table), channel_id=1, source_target_pairs={{0,12},{4,8},{8,4},{12,0},{16,28},{20,24},{24,20},{28,16},{1,13},{... | collective-permute-start | bytes 200 | tf_op jit(solution)/shard_map/ppermute | solution.py:153
  (5 other events, 48.2 us)

commit v2 on v1

--- a/solution.py
+++ b/solution.py
@@ -118,7 +118,6 @@
     return (losses, grad_queries, summed.astype(jnp.bfloat16))
 
 
-LOANS = (2, 1, 1)
 KERNEL_VMEM = 8 * 1024 * 1024
 NT = (((1,), (1,)), ((), ()))
 TN = (((0,), (0,)), ((), ()))
@@ -144,7 +143,8 @@
         and (block_total * shard_rows) % 256 == 0
         and block_total <= 4 * LIVE_MAX
         and block_total % 4 == 0
-        and sum(LOANS) == LIVE_MAX
+        and 2 * LIVE_MAX * shard_rows <= feature_width
+        and LIVE_MAX % 2 == 0
     )
 
 
@@ -156,6 +156,10 @@
 def inner(i):
     half = lax.axis_size("dp") // 2
     return (i // half + i // (half // 2)) % 2 == 1
+
+
+def outer(i):
+    return not inner(i)
 
 
 def far_rows(sources, at):
@@ -260,12 +264,12 @@
     send[...] = scores[pl.ds((1 - core) * slots, slots)]
 
 
-def lend_kernel(lists_of, first, table, *refs):
+def lend_kernel(lists_of, table, *refs):
     pieces, loan = refs[:-1], refs[-1]
     lists = lists_of(table)
-    for i in range(loan.shape[0]):
-        _, listed, _ = lists.slot(1, first + i)
-        loan[i] = listed_rows(pieces, listed)
+    for s in range(lists.slots):
+        _, listed, _ = lists.slot(1, s)
+        loan[s] = listed_rows(pieces, listed)
 
 
 def select_block(values, block):
@@ -328,11 +332,12 @@
 
 def weights_kernel(
     lists_of, scale, table, scores_in, scores_list, stats, far_stats, per_query, queries,
-    near_source, far_source, losses, weights_in, weights_own, weights_loan, *shares,
+    near_source, far_source, losses, weights_in, weights_own, weights_far, *shares,
 ):
     lists = lists_of(table)
     block_size = scores_list.shape[2]
-    shard_rows = shares[0].shape[1]
+    half_rows = weights_own.shape[1]
+    shard_rows = half_rows // len(shares)
     rows = [stats[i : i + 1, :] for i in range(5)]
     mirrored = [far_stats[i : i + 1, :] for i in range(5)]
     log_total = log_sum(rows[0:2], mirrored[2:4])
@@ -347,12 +352,20 @@
             * jnp.exp(scores_list[place] - select_block(logs[side], block)),
             0.0,
         ).astype(jnp.bfloat16)
-        (weights_loan if side else weights_own)[s] = weight
+        (weights_far if side else weights_own)[s] = weight
         at = pl.ds(block * block_size, block_size)
         share = scale * dot(weight, far_rows((near_source, far_source), at) if side else queries[at, :])
         share = share.astype(jnp.bfloat16)
         for k, out in enumerate(shares):
-            out[place] = share[k * shard_rows : (k + 1) * shard_rows]
+            out[place * shard_rows : (place + 1) * shard_rows] = share[
+                k * shard_rows : (k + 1) * shard_rows
+            ]
+    place_of = lax.broadcasted_iota(jnp.int32, (8, shares[0].shape[1]), 1) // shard_rows
+    ids = jnp.zeros(place_of.shape, jnp.float32)
+    for place, _, _, _, listed, _ in lists.sides():
+        ids = jnp.where(place_of == place, listed.astype(jnp.float32), ids)
+    for out in shares:
+        out[2 * lists.slots * shard_rows :] = ids.astype(jnp.bfloat16)
     near = scores_in[...]
     pos_column = per_query[1:2, :].astype(jnp.int32)
     is_positive = lax.broadcasted_iota(jnp.int32, near.shape, 0) == pos_column
@@ -368,7 +381,8 @@
 ):
     pieces, (query_total, own_part) = refs[:-2], refs[-2:]
     lists = lists_of(table)
-    block_size, shard_rows = weights_own.shape[2], own_share.shape[1]
+    block_size = weights_own.shape[2]
+    shard_rows = (own_share.shape[0] - 8) // (2 * lists.slots)
     near = weights_in[...]
     query_total[...] = dot(near, local[...], TN)
     own_part[...] = scale * dot(near, queries[...])
@@ -378,32 +392,37 @@
             at = pl.ds(block * block_size, block_size)
             query_total[at, :] = query_total[at, :] + dot(weights_own[s], rows, TN)
         at = pl.ds(listed * shard_rows, shard_rows)
-        own_part[at, :] = own_part[at, :] + own_share[place].astype(jnp.float32)
+        share = own_share[place * shard_rows : (place + 1) * shard_rows]
+        own_part[at, :] = own_part[at, :] + share.astype(jnp.float32)
 
 
 def far_grads_kernel(lists_of, scale, table, query_total, weights_far, *refs):
-    loans, (grad_queries, total) = refs[:-2], refs[-2:]
-    borrowed = [loan.at[i] for loan in loans for i in range(loan.shape[0])]
+    near_loan, far_loan, grad_queries, total = refs
     lists = lists_of(table)
     block_size = weights_far.shape[2]
+    is_inner = inner(lax.axis_index("dp"))
     total[...] = query_total[...]
-    for _, side, s, block, _, _ in lists.sides():
-        if not side:
-            at = pl.ds(block * block_size, block_size)
-            total[at, :] = total[at, :] + dot(weights_far[s], borrowed[s][...], TN)
+    for s in range(lists.slots):
+        block, _, _ = lists.slot(0, s)
+        rows = jnp.where(is_inner, near_loan[s], far_loan[s])
+        at = pl.ds(block * block_size, block_size)
+        total[at, :] = total[at, :] + dot(weights_far[s], rows, TN)
     grad_queries[...] = (scale * total[...]).astype(jnp.bfloat16)
 
 
-def collect_kernel(lists_of, own_part, *refs):
-    (*inputs, grad_passages, total), count = refs, (len(refs) - 2) // 2
-    tables, returned = inputs[:count], inputs[count:]
-    shard_rows = returned[0].shape[1]
-    total[...] = own_part[...]
-    for table, piece in zip(tables, returned):
-        for place, _, _, _, listed, _ in lists_of(table).sides():
-            at = pl.ds(listed * shard_rows, shard_rows)
-            total[at, :] = total[at, :] + piece[place].astype(jnp.float32)
-    grad_passages[...] = total[...].astype(jnp.bfloat16)
+def collect_kernel(shard_rows, own_part, *refs):
+    returned, grad_passages = refs[:-1], refs[-1]
+    total = own_part[...]
+    count = returned[0].shape[0] - 8
+    block = lax.broadcasted_iota(jnp.int32, (total.shape[0], count), 0)
+    place = lax.broadcasted_iota(jnp.int32, (total.shape[0], count), 1)
+    same_row = block % shard_rows == place % shard_rows
+    block = (block // shard_rows).astype(jnp.float32)
+    for piece in returned:
+        listed = piece[count:, :count][0:1].astype(jnp.float32)
+        chosen = jnp.where(same_row & (listed == block), 1.0, 0.0).astype(jnp.bfloat16)
+        total = total + dot(chosen, piece[:count])
+    grad_passages[...] = total.astype(jnp.bfloat16)
 
 
 def local_call(kernel, outs, scratch=(), hbm=()):
@@ -461,13 +480,10 @@
         else:
             by_peer[k] = [swap(chunk, "dp", low) for chunk in by_peer[k ^ low]]
     pieces = [chunk for k in range(half) for chunk in by_peer[k]]
-    far_queries = (
-        swap(queries, "dp", flip, inner), swap(queries, "dp", flip, lambda i: not inner(i))
-    )
+    far_queries = (swap(queries, "dp", flip, inner), swap(queries, "dp", flip, outer))
     mine = jnp.concatenate([list_lengths, block_lists.reshape(-1)])
     far_mine = swap(mine, "dp", flip)
     (table,) = local_call(join_kernel, [((2 * mine.shape[0],), jnp.int32)])(mine, far_mine)
-    tables = [swap(table, "dp", k) for k in peers]
     pos_column = positive // block_size * shard_rows + positive % block_size - me * shard_rows
     per_query = jnp.stack([loss_grad, pos_column.astype(f32)])
 
@@ -483,13 +499,10 @@
         scratch=[((2 * slots, half_rows, block_size), f32)],
     )(table, queries, *far_queries, *pieces)
 
-    borrowed = []
-    for i, count in enumerate(LOANS):
-        (loan,) = local_call(
-            functools.partial(lend_kernel, lists_of, sum(LOANS[:i])),
-            [((count, half_rows, width), bf16)],
-        )(table, *pieces)
-        borrowed.append(swap(loan, "dp", flip))
+    (loan,) = local_call(
+        functools.partial(lend_kernel, lists_of), [((slots, half_rows, width), bf16)]
+    )(table, *pieces)
+    borrowed = (swap(loan, "dp", flip, inner), swap(loan, "dp", flip, outer))
     list_sums = sum_over_grp(keep_list, send_list)
 
     scores_in, scores_list, stats = local_call(
@@ -503,15 +516,15 @@
     far_stats = swap_shared(stats, flip)
 
     weights_half = ((slots, half_rows, block_size), bf16)
-    piece = ((2 * slots, shard_rows, width), bf16)
+    piece = ((2 * slots * shard_rows + 8, width), bf16)
     losses, weights_in, weights_own, weights_loan, *shares = local_call(
         functools.partial(weights_kernel, lists_of, scale),
         [((1, query_rows), f32), ((own_rows, query_rows), bf16), weights_half, weights_half]
         + [piece] * half,
         hbm=(0,),
     )(table, scores_in, scores_list, stats, far_stats, per_query, queries, *far_queries)
-    returned = [swap(shares[k], "dp", k) for k in reversed(peers)][::-1]
-    weights_far = swap_shared(weights_loan, flip)
+    returned = [swap(shares[k], "dp", k) for k in reversed(peers)]
+    weights_far = swap(weights_loan, "dp", flip)
 
     query_total, own_part = local_call(
         functools.partial(own_grads_kernel, lists_of, scale),
@@ -524,11 +537,8 @@
         hbm=(0,),
     )(table, query_total, weights_far, *borrowed)
     (grad_passages,) = local_call(
-        functools.partial(collect_kernel, lists_of),
-        [((own_rows, width), bf16)],
-        scratch=[((own_rows, width), f32)],
-        hbm=(0,),
-    )(own_part, *tables, *returned)
+        functools.partial(collect_kernel, shard_rows), [((own_rows, width), bf16)], hbm=(0,)
+    )(own_part, *returned)
     return (
         losses.reshape(query_rows),
         grad_queries,

time: 101 us -> 98.1 us (0.971)
  waiting for transfers between devices: 46.4 us -> 39.4 us
  starting transfers between devices: 37.9 us -> 43 us
  Pallas kernels: 12 us -> 10.6 us
    ppermute x23 -> x20, waiting for transfers between devices: 43.3 us -> 31.2 us  [swap(): return lax.ppermute(value, axis, pairs)]
    ppermute x23 -> x20, starting transfers between devices: 35.2 us -> 40.9 us  [swap(): return lax.ppermute(value, axis, pairs)]
    ppermute x2 -> x1, waiting for transfers between devices: 3.1 us -> 8.25 us  [swap_shared(): return lax.ppermute(value, ('dp', 'grp'), pairs)]
    pallas_call x15 -> x13, Pallas kernels: 12 us -> 10.6 us  [call(): pl.pallas_call(kernel, out_shape=shapes, in_specs=[smem if table else vme...]
    ppermute x2 -> x1, starting transfers between devices: 2.7 us -> 2.07 us  [swap_shared(): return lax.ppermute(value, ('dp', 'grp'), pairs)]
  transfers between devices with their start and end apart: 25 -> 21, of which waited for: 9 -> 8; matrix products, arithmetic and copies ran while one was open for 2% -> 2% of each run, Pallas kernels for 10% -> 9%
where the time goes in v2:
time: 98.1 us; the launch traced here: 97.8 us
  starting transfers between devices  43 us (44%)
  waiting for transfers between devices  39.4 us (40%)
  Pallas kernels  10.6 us (11%)
  local copies, waits for them, and re-layouts  3.22 us (3%)
    ppermute x20, starting transfers between devices, swap(): return lax.ppermute(value, axis, pairs)  40.9 us
    ppermute x20, waiting for transfers between devices, swap(): return lax.ppermute(value, axis, pairs)  31.2 us
    pallas_call x13, Pallas kernels, call(): pl.pallas_call(kernel, out_shape=shapes, in_specs=[smem if table else vme...  10.6 us
    ppermute x1, waiting for transfers between devices, swap_shared(): return lax.ppermute(value, ('dp', 'grp'), pairs)  8.25 us
    ppermute x1, starting transfers between devices, swap_shared(): return lax.ppermute(value, ('dp', 'grp'), pairs)  2.07 us
  transfers between devices with their start and end apart: 21, of which 8 were waited for; matrix products, arithmetic and copies ran while one was open for 2% of the time, Pallas kernels for 9%

profile of v2, /device:TPU:0, one launch (start us, length us, event | category | flops | bytes accessed | tf_op | source)
XLA Modules:
  0.0 97.8 jit_solution(11152363441094082966)
XLA Ops:
  0.7 1.1 %slice.6 = bf16[12,16,1024]{2,1,0:T(8,128)(2,1)S(1)} slice(bf16[16,16,1024]{2,1,0:T(8,128)(2,1)} %refs_0_.3), slice={[0:12], [0:16], [0:1024]} | slice | bytes 786432 | tf_op jit(solution)/shard_map/slice | solution.py:472
  1.8 3.1 %collective-permute-start.7 = (bf16[12,16,1024]{2,1,0:T(8,128)(2,1)S(1)}, bf16[12,16,1024]{2,1,0:T(8,128)(2,1)S(1)}, u32[]{:S(2)}, u32[]{:S(2)}) collective-permute-start(bf16[12,16,1024]{2,1,0:T(8,128)(2,1)S(1)} %slice.6), channel_id=1, source_target_pairs={{0,8},{4,12},{8,0},{12,4},{16,24},{20,28},{24,16},{28,20},{1,9},{5... | collective-permute-start | bytes 1179656 | tf_op jit(solution)/shard_map/ppermute | solution.py:153
  4.9 1.5 %collective-permute-start.6 = (bf16[16,16,1024]{2,1,0:T(8,128)(2,1)S(1)}, bf16[16,16,1024]{2,1,0:T(8,128)(2,1)S(1)}, u32[]{:S(2)}, u32[]{:S(2)}) collective-permute-start(bf16[16,16,1024]{2,1,0:T(8,128)(2,1)S(1)} %copy-done), channel_id=1, source_target_pairs={{0,4},{4,0},{8,12},{12,8},{16,20},{20,16},{24,28},{28,24},{1,5},{5... | collective-permute-start | bytes 1572872 | tf_op jit(solution)/shard_map/ppermute | solution.py:153
  7.1 4.4 %collective-permute-start.5 = (bf16[256,1024]{1,0:T(8,128)(2,1)}, bf16[256,1024]{1,0:T(8,128)(2,1)S(1)}, u32[]{:S(2)}, u32[]{:S(2)}) collective-permute-start(bf16[256,1024]{1,0:T(8,128)(2,1)} %queries.7), channel_id=1, source_target_pairs={{0,24},{4,28},{24,0},{28,4},{1,25},{5,29},{25,1},{29,5},{2,26},{6,... | collective-permute-start | bytes 1572872 | tf_op jit(solution)/shard_map/ppermute | solution.py:153
  13.0 1.3 %collective-permute-start = (s32[8]{0:T(128)S(1)}, s32[8]{0:T(128)S(1)}, u32[]{:S(2)}, u32[]{:S(2)}) collective-permute-start(s32[8]{0:T(128)S(1)} %pad_add_fusion.a), channel_id=1, source_target_pairs={{0,24},{4,28},{8,16},{12,20},{16,8},{20,12},{24,0},{28,4},{1,25},{... | collective-permute-start | bytes 104 | tf_op jit(solution)/shard_map/ppermute | solution.py:153
  15.0 12.7 %collective-permute-done.b = s32[8]{0:T(128)S(1)} collective-permute-done((s32[8]{0:T(128)S(1)}, s32[8]{0:T(128)S(1)}, u32[]{:S(2)}, u32[]{:S(2)}) %collective-permute-start) | collective-permute-done | bytes 64 | tf_op jit(solution)/shard_map/ppermute | solution.py:153
  27.6 6.7 %collective-permute-start.8 = (bf16[4,16,1024]{2,1,0:T(8,128)(2,1)}, bf16[4,16,1024]{2,1,0:T(8,128)(2,1)S(1)}, u32[]{:S(2)}, u32[]{:S(2)}) collective-permute-start(bf16[4,16,1024]{2,1,0:T(8,128)(2,1)} %slice.7), channel_id=1, source_target_pairs={{0,8},{4,12},{8,0},{12,4},{16,24},{20,28},{24,16},{28,20},{1,9},{5... | collective-permute-start | bytes 393224 | tf_op jit(solution)/shard_map/ppermute | solution.py:153
  34.9 2.6 %collective-permute-done.8.refs_5_.refs_3_ = bf16[4,16,1024]{2,1,0:T(8,128)(2,1)S(1)} collective-permute-done((bf16[4,16,1024]{2,1,0:T(8,128)(2,1)}, bf16[4,16,1024]{2,1,0:T(8,128)(2,1)S(1)}, u32[]{:S(2)}, u32[]{:S(2)}) %collective-permute-start.8) | collective-permute-done | bytes 131104 | tf_op jit(solution)/shard_map/ppermute | solution.py:153
  39.2 1.1 %shard_map.85.table = s32[16]{0:T(128)S(1)} custom-call(s32[8]{0:T(128)S(1)} %pad_add_fusion.a, s32[8]{0:T(128)S(1)} %collective-permute-done.b), custom_call_target="tpu_custom_call" | custom-call | tf_op jit(solution)/shard_map/pallas_call | solution.py:441
  40.4 6.1 %collective-permute-done.10.refs_7_.refs_5_ = bf16[4,16,1024]{2,1,0:T(8,128)(2,1)S(1)} collective-permute-done((bf16[4,16,1024]{2,1,0:T(8,128)(2,1)S(1)}, bf16[4,16,1024]{2,1,0:T(8,128)(2,1)S(1)}, u32[]{:S(2)}, u32[]{:S(2)}) %collective-permute-start.10) | collective-permute-done | bytes 131104 | tf_op jit(solution)/shard_map/ppermute | solution.py:153
  46.5 1.4 %shard_map.89 = (f32[4,64,128]{2,1,0:T(8,128)S(1)}, f32[4,64,128]{2,1,0:T(8,128)S(1)}) custom-call(s32[16]{0:T(128)S(1)} %shard_map.85.table, bf16[256,1024]{1,0:T(8,128)(2,1)S(1)} %copy-done.1, bf16[256,1024]{1,0:T(8,128)(2,1)S(1)} %collective-permute-done.4.refs_0_.near_source, bf16[256,1024]{1,0:T(8,128)(2,1)S(1)} %collective-permute-done.5.refs_1_.far_source, ...), custom_call_target="tpu_custom_call" | custom-call | tf_op jit(solution)/shard_map/pallas_call | solution.py:441
  48.6 1.6 %collective-permute-start.2 = (f32[128,256]{1,0:T(8,128)S(1)}, f32[128,256]{1,0:T(8,128)S(1)}, u32[]{:S(2)}, u32[]{:S(2)}) collective-permute-start(f32[128,256]{1,0:T(8,128)S(1)} %shard_map.87.a), channel_id=1, source_target_pairs={{0,2},{1,3},{2,0},{3,1},{4,6},{5,7},{6,4},{7,5},{8,10},{9,11},{10,... | collective-permute-start | bytes 393224 | tf_op jit(solution)/shard_map/ppermute | solution.py:153
  52.5 4.3 %collective-permute-start.17 = (bf16[4,64,1024]{2,1,0:T(8,128)(2,1)S(1)}, bf16[4,64,1024]{2,1,0:T(8,128)(2,1)S(1)}, u32[]{:S(2)}, u32[]{:S(2)}) collective-permute-start(bf16[4,64,1024]{2,1,0:T(8,128)(2,1)S(1)} %shard_map.95), channel_id=1, source_target_pairs={{0,24},{4,28},{24,0},{28,4},{1,25},{5,29},{25,1},{29,5},{2,26},{6,... | collective-permute-start | bytes 1572872 | tf_op jit(solution)/shard_map/ppermute | solution.py:153
  59.1 2.1 %collective-permute-start.14 = (f32[8,256]{1,0:T(8,128)S(1)}, f32[8,256]{1,0:T(8,128)S(1)}, u32[]{:S(2)}, u32[]{:S(2)}) collective-permute-start(f32[8,256]{1,0:T(8,128)S(1)} %get-tuple-element.26.stats), channel_id=1, source_target_pairs={{0,25},{1,24},{2,27},{3,26},{4,29},{5,28},{6,31},{7,30},{8,17},{9,... | collective-permute-start | bytes 24584 | tf_op jit(solution)/shard_map/ppermute | solution.py:177
  61.2 8.2 %collective-permute-done.14.far_stats = f32[8,256]{1,0:T(8,128)S(1)} collective-permute-done((f32[8,256]{1,0:T(8,128)S(1)}, f32[8,256]{1,0:T(8,128)S(1)}, u32[]{:S(2)}, u32[]{:S(2)}) %collective-permute-start.14) | collective-permute-done | bytes 8224 | tf_op jit(solution)/shard_map/ppermute | solution.py:177
  69.5 1.6 %shard_map.93 = (f32[1,256]{1,0:T(1,128)}, bf16[256,256]{1,0:T(8,128)(2,1)S(1)}, bf16[4,64,128]{2,1,0:T(8,128)(2,1)S(1)}, bf16[4,64,128]{2,1,0:T(8,128)(2,1)S(1)...) custom-call(s32[16]{0:T(128)S(1)} %shard_map.85.table, ...), custom_call_target="tpu_custom_call" | custom-call | tf_op jit(solution)/shard_map/pallas_call | solution.py:441
  71.0 2.4 %collective-permute-start.15 = (bf16[4,64,128]{2,1,0:T(8,128)(2,1)S(1)}, bf16[4,64,128]{2,1,0:T(8,128)(2,1)S(1)}, u32[]{:S(2)}, u32[]{:S(2)}) collective-permute-start(bf16[4,64,128]{2,1,0:T(8,128)(2,1)S(1)} %get-tuple-element.32), channel_id=1, source_target_pairs={{0,24},{4,28},{8,16},{12,20},{16,8},{20,12},{24,0},{28,4},{1,25},{... | collective-permute-start | bytes 196616 | tf_op jit(solution)/shard_map/ppermute | solution.py:153
  73.4 9.6 %collective-permute-start.18 = (bf16[136,1024]{1,0:T(8,128)(2,1)S(1)}, bf16[136,1024]{1,0:T(8,128)(2,1)S(1)}, u32[]{:S(2)}, u32[]{:S(2)}) collective-permute-start(bf16[136,1024]{1,0:T(8,128)(2,1)S(1)} %get-tuple-element.34), channel_id=1, source_target_pairs={{0,12},{4,8},{8,4},{12,0},{16,28},{20,24},{24,20},{28,16},{1,13},{... | collective-permute-start | bytes 835592 | tf_op jit(solution)/shard_map/ppermute | solution.py:153
  83.0 1.5 %collective-permute-start.20 = (bf16[136,1024]{1,0:T(8,128)(2,1)S(1)}, bf16[136,1024]{1,0:T(8,128)(2,1)S(1)}, u32[]{:S(2)}, u32[]{:S(2)}) collective-permute-start(bf16[136,1024]{1,0:T(8,128)(2,1)S(1)} %get-tuple-element.36), channel_id=1, source_target_pairs={{0,4},{4,0},{8,12},{12,8},{16,20},{20,16},{24,28},{28,24},{1,5},{5... | collective-permute-start | bytes 835592 | tf_op jit(solution)/shard_map/ppermute | solution.py:153
  84.5 1.3 %shard_map.94 = (f32[256,1024]{1,0:T(8,128)S(1)}, f32[256,1024]{1,0:T(8,128)S(1)}) custom-call(s32[16]{0:T(128)S(1)} %shard_map.85.table, bf16[256,256]{1,0:T(8,128)(2,1)S(1)} %get-tuple-element.28.weights_in, bf16[4,64,128]{2,1,0:T(8,128)(2,1)S(1)} %get-tuple-element.29.weights_own, bf16[256,1024]{1,0:T(8,128)(2,1)S(1)} %copy-done.1, ...), custom_call_target="tpu_custom_call" | custom-call | tf_op jit(solution)/shard_map/pallas_call | solution.py:441
  85.8 1.9 %shard_map.96 = bf16[256,1024]{1,0:T(8,128)(2,1)} custom-call(s32[16]{0:T(128)S(1)} %shard_map.85.table, f32[256,1024]{1,0:T(8,128)S(1)} %get-tuple-element.31.query_total, bf16[4,64,128]{2,1,0:T(8,128)(2,1)S(1)} %collective-permute-done.15.weights_far, bf16[4,64,1024]{2,1,0:T(8,128)(2,1)S(1)} %collective-permute-done.16.refs_0_, ...), custom_call_target="tpu_custom_call" | custom-call | tf_op jit(solution)/shard_map/pallas_call | solution.py:441
  87.7 2.8 %collective-permute-done.18.refs_0_ = bf16[136,1024]{1,0:T(8,128)(2,1)S(1)} collective-permute-done((bf16[136,1024]{1,0:T(8,128)(2,1)S(1)}, bf16[136,1024]{1,0:T(8,128)(2,1)S(1)}, u32[]{:S(2)}, u32[]{:S(2)}) %collective-permute-start.18) | collective-permute-done | bytes 278560 | tf_op jit(solution)/shard_map/ppermute | solution.py:153
  90.5 5.9 %collective-permute-done.19.refs_1_ = bf16[136,1024]{1,0:T(8,128)(2,1)S(1)} collective-permute-done((bf16[136,1024]{1,0:T(8,128)(2,1)S(1)}, bf16[136,1024]{1,0:T(8,128)(2,1)S(1)}, u32[]{:S(2)}, u32[]{:S(2)}) %collective-permute-start.19) | collective-permute-done | bytes 278560 | tf_op jit(solution)/shard_map/ppermute | solution.py:153
  96.4 1.4 %shard_map.97 = bf16[256,1024]{1,0:T(8,128)(2,1)} custom-call(f32[256,1024]{1,0:T(8,128)S(1)} %get-tuple-element.33.own_part, bf16[136,1024]{1,0:T(8,128)(2,1)S(1)} %collective-permute-done.18.refs_0_, bf16[136,1024]{1,0:T(8,128)(2,1)S(1)} %collective-permute-done.19.refs_1_, bf16[136,1024]{1,0:T(8,128)(2,1)S(1)} %collective-permute-done.20.refs_2_), custom_call_target="tpu_custom_call" | custom-call | tf_op jit(solution)/shard_map/pallas_call | solution.py:441
  (45 shorter events, 10.4 us)
Async XLA Ops:
  0.6 4.3 %copy-start = (bf16[16,16,1024]{2,1,0:T(8,128)(2,1)S(1)}, bf16[16,16,1024]{2,1,0:T(8,128)(2,1)}, u32[]{:S(2)}) copy-start(bf16[16,16,1024]{2,1,0:T(8,128)(2,1)} %refs_0_.3) | copy-start | bytes 1572868
  0.6 38.1 %copy-start.1 = (bf16[256,1024]{1,0:T(8,128)(2,1)S(1)}, bf16[256,1024]{1,0:T(8,128)(2,1)}, u32[]{:S(2)}) copy-start(bf16[256,1024]{1,0:T(8,128)(2,1)} %queries.7) | copy-start | bytes 1572868
  1.8 32.6 %collective-permute-start.7 = (bf16[12,16,1024]{2,1,0:T(8,128)(2,1)S(1)}, bf16[12,16,1024]{2,1,0:T(8,128)(2,1)S(1)}, u32[]{:S(2)}, u32[]{:S(2)}) collective-permute-start(bf16[12,16,1024]{2,1,0:T(8,128)(2,1)S(1)} %slice.6), channel_id=1, source_target_pairs={{0,8},{4,12},{8,0},{12,4},{16,24},{20,28},{24,16},{28,20},{1,9},{5... | collective-permute-start | bytes 1179656 | tf_op jit(solution)/shard_map/ppermute | solution.py:153
  4.9 41.6 %collective-permute-start.6 = (bf16[16,16,1024]{2,1,0:T(8,128)(2,1)S(1)}, bf16[16,16,1024]{2,1,0:T(8,128)(2,1)S(1)}, u32[]{:S(2)}, u32[]{:S(2)}) collective-permute-start(bf16[16,16,1024]{2,1,0:T(8,128)(2,1)S(1)} %copy-done), channel_id=1, source_target_pairs={{0,4},{4,0},{8,12},{12,8},{16,20},{20,16},{24,28},{28,24},{1,5},{5... | collective-permute-start | bytes 1572872 | tf_op jit(solution)/shard_map/ppermute | solution.py:153
  6.4 40.1 %collective-permute-start.4 = (bf16[256,1024]{1,0:T(8,128)(2,1)}, bf16[256,1024]{1,0:T(8,128)(2,1)S(1)}, u32[]{:S(2)}, u32[]{:S(2)}) collective-permute-start(bf16[256,1024]{1,0:T(8,128)(2,1)} %queries.7), channel_id=1, source_target_pairs={{8,16},{12,20},{16,8},{20,12},{9,17},{13,21},{17,9},{21,13},{10,18... | collective-permute-start | bytes 1572872 | tf_op jit(solution)/shard_map/ppermute | solution.py:153
  7.1 39.5 %collective-permute-start.5 = (bf16[256,1024]{1,0:T(8,128)(2,1)}, bf16[256,1024]{1,0:T(8,128)(2,1)S(1)}, u32[]{:S(2)}, u32[]{:S(2)}) collective-permute-start(bf16[256,1024]{1,0:T(8,128)(2,1)} %queries.7), channel_id=1, source_target_pairs={{0,24},{4,28},{24,0},{28,4},{1,25},{5,29},{25,1},{29,5},{2,26},{6,... | collective-permute-start | bytes 1572872 | tf_op jit(solution)/shard_map/ppermute | solution.py:153
  13.0 14.7 %collective-permute-start = (s32[8]{0:T(128)S(1)}, s32[8]{0:T(128)S(1)}, u32[]{:S(2)}, u32[]{:S(2)}) collective-permute-start(s32[8]{0:T(128)S(1)} %pad_add_fusion.a), channel_id=1, source_target_pairs={{0,24},{4,28},{8,16},{12,20},{16,8},{20,12},{24,0},{28,4},{1,25},{... | collective-permute-start | bytes 104 | tf_op jit(solution)/shard_map/ppermute | solution.py:153
  27.6 9.9 %collective-permute-start.8 = (bf16[4,16,1024]{2,1,0:T(8,128)(2,1)}, bf16[4,16,1024]{2,1,0:T(8,128)(2,1)S(1)}, u32[]{:S(2)}, u32[]{:S(2)}) collective-permute-start(bf16[4,16,1024]{2,1,0:T(8,128)(2,1)} %slice.7), channel_id=1, source_target_pairs={{0,8},{4,12},{8,0},{12,4},{16,24},{20,28},{24,16},{28,20},{1,9},{5... | collective-permute-start | bytes 393224 | tf_op jit(solution)/shard_map/ppermute | solution.py:153
  34.3 12.2 %collective-permute-start.9 = (bf16[12,16,1024]{2,1,0:T(8,128)(2,1)S(1)}, bf16[12,16,1024]{2,1,0:T(8,128)(2,1)S(1)}, u32[]{:S(2)}, u32[]{:S(2)}) collective-permute-start(bf16[12,16,1024]{2,1,0:T(8,128)(2,1)S(1)} %collective-permute-done.7.refs_4_.refs_2_), channel_id=1, source_target_pairs={{0,4},{4,0},{8,12},{12,8},{16,20},{20,16},{24,28},{28,24},{1,5},{5... | collective-permute-start | bytes 1179656 | tf_op jit(solution)/shard_map/ppermute | solution.py:153
  34.9 3.2 %copy-start.2 = (s32[256]{0:T(256)S(1)}, s32[256]{0:T(256)}, u32[]{:S(2)}) copy-start(s32[256]{0:T(256)} %param.10) | copy-start | bytes 3076
  37.5 9.0 %collective-permute-start.10 = (bf16[4,16,1024]{2,1,0:T(8,128)(2,1)S(1)}, bf16[4,16,1024]{2,1,0:T(8,128)(2,1)S(1)}, u32[]{:S(2)}, u32[]{:S(2)}) collective-permute-start(bf16[4,16,1024]{2,1,0:T(8,128)(2,1)S(1)} %collective-permute-done.8.refs_5_.refs_3_), channel_id=1, source_target_pairs={{0,4},{4,0},{8,12},{12,8},{16,20},{20,16},{24,28},{28,24},{1,5},{5... | collective-permute-start | bytes 393224 | tf_op jit(solution)/shard_map/ppermute | solution.py:153
  46.5 2.0 %collective-permute-start.1 = (f32[128,256]{1,0:T(8,128)S(1)}, f32[128,256]{1,0:T(8,128)S(1)}, u32[]{:S(2)}, u32[]{:S(2)}) collective-permute-start(f32[128,256]{1,0:T(8,128)S(1)} %get-tuple-element.21), channel_id=1, source_target_pairs={{0,1},{1,0},{2,3},{3,2},{4,5},{5,4},{6,7},{7,6},{8,9},{9,8},{10,11... | collective-permute-start | bytes 393224 | tf_op jit(solution)/shard_map/ppermute | solution.py:153
  48.0 2.2 %collective-permute-start.11 = (f32[4,64,128]{2,1,0:T(8,128)S(1)}, f32[4,64,128]{2,1,0:T(8,128)S(1)}, u32[]{:S(2)}, u32[]{:S(2)}) collective-permute-start(f32[4,64,128]{2,1,0:T(8,128)S(1)} %get-tuple-element.23), channel_id=1, source_target_pairs={{0,1},{1,0},{2,3},{3,2},{4,5},{5,4},{6,7},{7,6},{8,9},{9,8},{10,11... | collective-permute-start | bytes 393224 | tf_op jit(solution)/shard_map/ppermute | solution.py:153
  48.6 8.2 %collective-permute-start.2 = (f32[128,256]{1,0:T(8,128)S(1)}, f32[128,256]{1,0:T(8,128)S(1)}, u32[]{:S(2)}, u32[]{:S(2)}) collective-permute-start(f32[128,256]{1,0:T(8,128)S(1)} %shard_map.87.a), channel_id=1, source_target_pairs={{0,2},{1,3},{2,0},{3,1},{4,6},{5,7},{6,4},{7,5},{8,10},{9,11},{10,... | collective-permute-start | bytes 393224 | tf_op jit(solution)/shard_map/ppermute | solution.py:153
  50.2 6.7 %collective-permute-start.12 = (f32[4,64,128]{2,1,0:T(8,128)S(1)}, f32[4,64,128]{2,1,0:T(8,128)S(1)}, u32[]{:S(2)}, u32[]{:S(2)}) collective-permute-start(f32[4,64,128]{2,1,0:T(8,128)S(1)} %shard_map.90.a), channel_id=1, source_target_pairs={{0,2},{1,3},{2,0},{3,1},{4,6},{5,7},{6,4},{7,5},{8,10},{9,11},{10,... | collective-permute-start | bytes 393224 | tf_op jit(solution)/shard_map/ppermute | solution.py:153
  51.8 34.0 %collective-permute-start.16 = (bf16[4,64,1024]{2,1,0:T(8,128)(2,1)S(1)}, bf16[4,64,1024]{2,1,0:T(8,128)(2,1)S(1)}, u32[]{:S(2)}, u32[]{:S(2)}) collective-permute-start(bf16[4,64,1024]{2,1,0:T(8,128)(2,1)S(1)} %shard_map.95), channel_id=1, source_target_pairs={{8,16},{12,20},{16,8},{20,12},{9,17},{13,21},{17,9},{21,13},{10,18... | collective-permute-start | bytes 1572872 | tf_op jit(solution)/shard_map/ppermute | solution.py:153
  52.5 33.3 %collective-permute-start.17 = (bf16[4,64,1024]{2,1,0:T(8,128)(2,1)S(1)}, bf16[4,64,1024]{2,1,0:T(8,128)(2,1)S(1)}, u32[]{:S(2)}, u32[]{:S(2)}) collective-permute-start(bf16[4,64,1024]{2,1,0:T(8,128)(2,1)S(1)} %shard_map.95), channel_id=1, source_target_pairs={{0,24},{4,28},{24,0},{28,4},{1,25},{5,29},{25,1},{29,5},{2,26},{6,... | collective-permute-start | bytes 1572872 | tf_op jit(solution)/shard_map/ppermute | solution.py:153
  56.8 1.4 %collective-permute-start.3 = (f32[128,256]{1,0:T(8,128)S(1)}, f32[128,256]{1,0:T(8,128)S(1)}, u32[]{:S(2)}, u32[]{:S(2)}) collective-permute-start(f32[128,256]{1,0:T(8,128)S(1)} %shard_map.88.in_half), channel_id=1, source_target_pairs={{0,1},{1,0},{2,3},{3,2},{4,5},{5,4},{6,7},{7,6},{8,9},{9,8},{10,11... | collective-permute-start | bytes 393224 | tf_op jit(solution)/shard_map/ppermute | solution.py:153
  56.9 1.5 %collective-permute-start.13 = (f32[4,64,128]{2,1,0:T(8,128)S(1)}, f32[4,64,128]{2,1,0:T(8,128)S(1)}, u32[]{:S(2)}, u32[]{:S(2)}) collective-permute-start(f32[4,64,128]{2,1,0:T(8,128)S(1)} %shard_map.91.list_half), channel_id=1, source_target_pairs={{0,1},{1,0},{2,3},{3,2},{4,5},{5,4},{6,7},{7,6},{8,9},{9,8},{10,11... | collective-permute-start | bytes 393224 | tf_op jit(solution)/shard_map/ppermute | solution.py:153
  59.1 10.3 %collective-permute-start.14 = (f32[8,256]{1,0:T(8,128)S(1)}, f32[8,256]{1,0:T(8,128)S(1)}, u32[]{:S(2)}, u32[]{:S(2)}) collective-permute-start(f32[8,256]{1,0:T(8,128)S(1)} %get-tuple-element.26.stats), channel_id=1, source_target_pairs={{0,25},{1,24},{2,27},{3,26},{4,29},{5,28},{6,31},{7,30},{8,17},{9,... | collective-permute-start | bytes 24584 | tf_op jit(solution)/shard_map/ppermute | solution.py:177
  71.0 12.0 %collective-permute-start.15 = (bf16[4,64,128]{2,1,0:T(8,128)(2,1)S(1)}, bf16[4,64,128]{2,1,0:T(8,128)(2,1)S(1)}, u32[]{:S(2)}, u32[]{:S(2)}) collective-permute-start(bf16[4,64,128]{2,1,0:T(8,128)(2,1)S(1)} %get-tuple-element.32), channel_id=1, source_target_pairs={{0,24},{4,28},{8,16},{12,20},{16,8},{20,12},{24,0},{28,4},{1,25},{... | collective-permute-start | bytes 196616 | tf_op jit(solution)/shard_map/ppermute | solution.py:153
  73.4 17.1 %collective-permute-start.18 = (bf16[136,1024]{1,0:T(8,128)(2,1)S(1)}, bf16[136,1024]{1,0:T(8,128)(2,1)S(1)}, u32[]{:S(2)}, u32[]{:S(2)}) collective-permute-start(bf16[136,1024]{1,0:T(8,128)(2,1)S(1)} %get-tuple-element.34), channel_id=1, source_target_pairs={{0,12},{4,8},{8,4},{12,0},{16,28},{20,24},{24,20},{28,16},{1,13},{... | collective-permute-start | bytes 835592 | tf_op jit(solution)/shard_map/ppermute | solution.py:153
  83.0 13.5 %collective-permute-start.19 = (bf16[136,1024]{1,0:T(8,128)(2,1)S(1)}, bf16[136,1024]{1,0:T(8,128)(2,1)S(1)}, u32[]{:S(2)}, u32[]{:S(2)}) collective-permute-start(bf16[136,1024]{1,0:T(8,128)(2,1)S(1)} %get-tuple-element.35), channel_id=1, source_target_pairs={{0,8},{4,12},{8,0},{12,4},{16,24},{20,28},{24,16},{28,20},{1,9},{5... | collective-permute-start | bytes 835592 | tf_op jit(solution)/shard_map/ppermute | solution.py:153
  83.0 13.5 %collective-permute-start.20 = (bf16[136,1024]{1,0:T(8,128)(2,1)S(1)}, bf16[136,1024]{1,0:T(8,128)(2,1)S(1)}, u32[]{:S(2)}, u32[]{:S(2)}) collective-permute-start(bf16[136,1024]{1,0:T(8,128)(2,1)S(1)} %get-tuple-element.36), channel_id=1, source_target_pairs={{0,4},{4,0},{8,12},{12,8},{16,20},{20,16},{24,28},{28,24},{1,5},{5... | collective-permute-start | bytes 835592 | tf_op jit(solution)/shard_map/ppermute | solution.py:153
  (1 other events, 0.7 us)

commit v3 on v2

--- a/solution.py
+++ b/solution.py
@@ -142,7 +142,7 @@
         and feature_width % 128 == 0
         and (block_total * shard_rows) % 256 == 0
         and block_total <= 4 * LIVE_MAX
-        and block_total % 4 == 0
+        and block_total % 8 == 0
         and 2 * LIVE_MAX * shard_rows <= feature_width
         and LIVE_MAX % 2 == 0
     )
@@ -331,8 +331,8 @@
 
 
 def weights_kernel(
-    lists_of, scale, table, scores_in, scores_list, stats, far_stats, per_query, queries,
-    near_source, far_source, losses, weights_in, weights_own, weights_far, *shares,
+    lists_of, scale, table, scores_list, stats, far_stats, queries, near_source, far_source,
+    weights_own, weights_far, *shares,
 ):
     lists = lists_of(table)
     block_size = scores_list.shape[2]
@@ -366,24 +366,26 @@
         ids = jnp.where(place_of == place, listed.astype(jnp.float32), ids)
     for out in shares:
         out[2 * lists.slots * shard_rows :] = ids.astype(jnp.bfloat16)
-    near = scores_in[...]
-    pos_column = per_query[1:2, :].astype(jnp.int32)
-    is_positive = lax.broadcasted_iota(jnp.int32, near.shape, 0) == pos_column
-    positive_score = jnp.sum(jnp.where(is_positive, near, 0.0), axis=0, keepdims=True)
-    losses[...] = log_total - positive_score
-    weights_in[...] = (
-        grad * (jnp.exp(near - log_total) - is_positive.astype(jnp.float32))
-    ).astype(jnp.bfloat16)
 
 
 def own_grads_kernel(
-    lists_of, scale, table, weights_in, weights_own, queries, local, own_share, *refs
+    lists_of, scale, table, scores_in, stats, far_stats, per_query, weights_own, queries, local,
+    own_share, *refs,
 ):
-    pieces, (query_total, own_part) = refs[:-2], refs[-2:]
+    pieces, (losses, query_total, own_part) = refs[:-3], refs[-3:]
     lists = lists_of(table)
     block_size = weights_own.shape[2]
     shard_rows = (own_share.shape[0] - 8) // (2 * lists.slots)
-    near = weights_in[...]
+    rows = [stats[i : i + 1, :] for i in range(5)]
+    log_total = log_sum(rows[0:2], [far_stats[i : i + 1, :] for i in range(2, 4)])
+    scores = scores_in[...]
+    pos_column = per_query[1:2, :].astype(jnp.int32)
+    is_positive = lax.broadcasted_iota(jnp.int32, scores.shape, 0) == pos_column
+    positive_score = jnp.sum(jnp.where(is_positive, scores, 0.0), axis=0, keepdims=True)
+    losses[...] = log_total - positive_score
+    near = (
+        rows[4] * (jnp.exp(scores - log_total) - is_positive.astype(jnp.float32))
+    ).astype(jnp.bfloat16)
     query_total[...] = dot(near, local[...], TN)
     own_part[...] = scale * dot(near, queries[...])
     for place, side, s, block, listed, _ in lists.sides():
@@ -468,7 +470,7 @@
         Lists, block_count=block_count, list_cap=list_cap, slots=slots
     )
 
-    cut_at = block_total * 3 // 4
+    cut_at = block_total * 5 // 8
     chunks = [passages[:cut_at], passages[cut_at:]]
     by_peer = {0: [passages]}
     for k in sorted(peers, key=lambda k: (k.bit_count(), -k)):
@@ -517,19 +519,21 @@
 
     weights_half = ((slots, half_rows, block_size), bf16)
     piece = ((2 * slots * shard_rows + 8, width), bf16)
-    losses, weights_in, weights_own, weights_loan, *shares = local_call(
+    weights_own, weights_loan, *shares = local_call(
         functools.partial(weights_kernel, lists_of, scale),
-        [((1, query_rows), f32), ((own_rows, query_rows), bf16), weights_half, weights_half]
-        + [piece] * half,
-        hbm=(0,),
-    )(table, scores_in, scores_list, stats, far_stats, per_query, queries, *far_queries)
+        [weights_half, weights_half] + [piece] * half,
+    )(table, scores_list, stats, far_stats, queries, *far_queries)
     returned = [swap(shares[k], "dp", k) for k in reversed(peers)]
     weights_far = swap(weights_loan, "dp", flip)
 
-    query_total, own_part = local_call(
+    losses, query_total, own_part = local_call(
         functools.partial(own_grads_kernel, lists_of, scale),
-        [((query_rows, width), f32), ((own_rows, width), f32)],
-    )(table, weights_in, weights_own, queries, local, shares[0], *pieces)
+        [((1, query_rows), f32), ((query_rows, width), f32), ((own_rows, width), f32)],
+        hbm=(0,),
+    )(
+        table, scores_in, stats, far_stats, per_query, weights_own, queries, local, shares[0],
+        *pieces,
+    )
     (grad_queries,) = local_call(
         functools.partial(far_grads_kernel, lists_of, scale),
         [((query_rows, width), bf16)],

time: 98.1 us -> 86.5 us (0.88)
  waiting for transfers between devices: 39.4 us -> 33.6 us
  starting transfers between devices: 43 us -> 38 us
    ppermute x20, waiting for transfers between devices: 31.2 us -> 25.2 us  [swap(): return lax.ppermute(value, axis, pairs)]
    ppermute x20, starting transfers between devices: 40.9 us -> 36.4 us  [swap(): return lax.ppermute(value, axis, pairs)]
  transfers between devices with their start and end apart: 21 -> 21, of which waited for: 8 -> 9; matrix products, arithmetic and copies ran while one was open for 2% -> 2% of each run, Pallas kernels for 9% -> 11%
where the time goes in v3:
time: 86.5 us; the launch traced here: 86.3 us
  starting transfers between devices  38 us (44%)
  waiting for transfers between devices  33.6 us (39%)
  Pallas kernels  10.6 us (12%)
  local copies, waits for them, and re-layouts  3.22 us (4%)
    ppermute x20, starting transfers between devices, swap(): return lax.ppermute(value, axis, pairs)  36.4 us
    ppermute x20, waiting for transfers between devices, swap(): return lax.ppermute(value, axis, pairs)  25.2 us
    pallas_call x13, Pallas kernels, call(): pl.pallas_call(kernel, out_shape=shapes, in_specs=[smem if table else vme...  10.6 us
    ppermute x1, waiting for transfers between devices, swap_shared(): return lax.ppermute(value, ('dp', 'grp'), pairs)  8.33 us
    slice x2, local copies, waits for them, and re-layouts, mirror_plan(): chunks = [passages[:cut_at], passages[cut_at:]]  1.77 us
  transfers between devices with their start and end apart: 21, of which 9 were waited for; matrix products, arithmetic and copies ran while one was open for 2% of the time, Pallas kernels for 11%

profile of v3, /device:TPU:0, one launch (start us, length us, event | category | flops | bytes accessed | tf_op | source)
XLA Modules:
  0.0 86.3 jit_solution(8537104130291305242)
XLA Ops:
  0.6 1.1 %slice.6 = bf16[10,16,1024]{2,1,0:T(8,128)(2,1)S(1)} slice(bf16[16,16,1024]{2,1,0:T(8,128)(2,1)} %refs_0_.3), slice={[0:10], [0:16], [0:1024]} | slice | bytes 655360 | tf_op jit(solution)/shard_map/slice | solution.py:474
  1.7 3.1 %collective-permute-start.7 = (bf16[10,16,1024]{2,1,0:T(8,128)(2,1)S(1)}, bf16[10,16,1024]{2,1,0:T(8,128)(2,1)S(1)}, u32[]{:S(2)}, u32[]{:S(2)}) collective-permute-start(bf16[10,16,1024]{2,1,0:T(8,128)(2,1)S(1)} %slice.6), channel_id=1, source_target_pairs={{0,8},{4,12},{8,0},{12,4},{16,24},{20,28},{24,16},{28,20},{1,9},{5... | collective-permute-start | bytes 983048 | tf_op jit(solution)/shard_map/ppermute | solution.py:153
  4.9 1.5 %collective-permute-start.6 = (bf16[16,16,1024]{2,1,0:T(8,128)(2,1)S(1)}, bf16[16,16,1024]{2,1,0:T(8,128)(2,1)S(1)}, u32[]{:S(2)}, u32[]{:S(2)}) collective-permute-start(bf16[16,16,1024]{2,1,0:T(8,128)(2,1)S(1)} %copy-done), channel_id=1, source_target_pairs={{0,4},{4,0},{8,12},{12,8},{16,20},{20,16},{24,28},{28,24},{1,5},{5... | collective-permute-start | bytes 1572872 | tf_op jit(solution)/shard_map/ppermute | solution.py:153
  8.3 3.6 %collective-permute-start = (s32[8]{0:T(128)S(1)}, s32[8]{0:T(128)S(1)}, u32[]{:S(2)}, u32[]{:S(2)}) collective-permute-start(s32[8]{0:T(128)S(1)} %pad_add_fusion.a), channel_id=1, source_target_pairs={{0,24},{4,28},{8,16},{12,20},{16,8},{20,12},{24,0},{28,4},{1,25},{... | collective-permute-start | bytes 104 | tf_op jit(solution)/shard_map/ppermute | solution.py:153
  12.6 6.4 %collective-permute-done.b = s32[8]{0:T(128)S(1)} collective-permute-done((s32[8]{0:T(128)S(1)}, s32[8]{0:T(128)S(1)}, u32[]{:S(2)}, u32[]{:S(2)}) %collective-permute-start) | collective-permute-done | bytes 64 | tf_op jit(solution)/shard_map/ppermute | solution.py:153
  19.0 3.2 %collective-permute-start.5 = (bf16[256,1024]{1,0:T(8,128)(2,1)S(1)}, bf16[256,1024]{1,0:T(8,128)(2,1)S(1)}, u32[]{:S(2)}, u32[]{:S(2)}) collective-permute-start(bf16[256,1024]{1,0:T(8,128)(2,1)S(1)} %copy-done.1), channel_id=1, source_target_pairs={{0,24},{4,28},{24,0},{28,4},{1,25},{5,29},{25,1},{29,5},{2,26},{6,... | collective-permute-start | bytes 1572872 | tf_op jit(solution)/shard_map/ppermute | solution.py:153
  22.3 1.6 %collective-permute-start.10 = (bf16[6,16,1024]{2,1,0:T(8,128)(2,1)S(1)}, bf16[6,16,1024]{2,1,0:T(8,128)(2,1)S(1)}, u32[]{:S(2)}, u32[]{:S(2)}) collective-permute-start(bf16[6,16,1024]{2,1,0:T(8,128)(2,1)S(1)} %collective-permute-done.8.refs_5_.refs_3_), channel_id=1, source_target_pairs={{0,4},{4,0},{8,12},{12,8},{16,20},{20,16},{24,28},{28,24},{1,5},{5... | collective-permute-start | bytes 589832 | tf_op jit(solution)/shard_map/ppermute | solution.py:153
  25.5 1.1 %shard_map.85.table = s32[16]{0:T(128)S(1)} custom-call(s32[8]{0:T(128)S(1)} %pad_add_fusion.a, s32[8]{0:T(128)S(1)} %collective-permute-done.b), custom_call_target="tpu_custom_call" | custom-call | tf_op jit(solution)/shard_map/pallas_call | solution.py:443
  26.7 3.4 %collective-permute-done.10.refs_7_.refs_5_ = bf16[6,16,1024]{2,1,0:T(8,128)(2,1)S(1)} collective-permute-done((bf16[6,16,1024]{2,1,0:T(8,128)(2,1)S(1)}, bf16[6,16,1024]{2,1,0:T(8,128)(2,1)S(1)}, u32[]{:S(2)}, u32[]{:S(2)}) %collective-permute-start.10) | collective-permute-done | bytes 196640 | tf_op jit(solution)/shard_map/ppermute | solution.py:153
  30.1 5.2 %collective-permute-done.5.refs_1_.far_source = bf16[256,1024]{1,0:T(8,128)(2,1)S(1)} collective-permute-done((bf16[256,1024]{1,0:T(8,128)(2,1)S(1)}, bf16[256,1024]{1,0:T(8,128)(2,1)S(1)}, u32[]{:S(2)}, u32[]{:S(2)}) %collective-permute-start.5) | collective-permute-done | bytes 524320 | tf_op jit(solution)/shard_map/ppermute | solution.py:153
  35.3 1.4 %shard_map.89 = (f32[4,64,128]{2,1,0:T(8,128)S(1)}, f32[4,64,128]{2,1,0:T(8,128)S(1)}) custom-call(s32[16]{0:T(128)S(1)} %shard_map.85.table, bf16[256,1024]{1,0:T(8,128)(2,1)S(1)} %copy-done.1, bf16[256,1024]{1,0:T(8,128)(2,1)S(1)} %collective-permute-done.4.refs_0_.near_source, bf16[256,1024]{1,0:T(8,128)(2,1)S(1)} %collective-permute-done.5.refs_1_.far_source, ...), custom_call_target="tpu_custom_call" | custom-call | tf_op jit(solution)/shard_map/pallas_call | solution.py:443
  36.8 1.6 %collective-permute-start.2 = (f32[128,256]{1,0:T(8,128)S(1)}, f32[128,256]{1,0:T(8,128)S(1)}, u32[]{:S(2)}, u32[]{:S(2)}) collective-permute-start(f32[128,256]{1,0:T(8,128)S(1)} %shard_map.87.a), channel_id=1, source_target_pairs={{0,2},{1,3},{2,0},{3,1},{4,6},{5,7},{6,4},{7,5},{8,10},{9,11},{10,... | collective-permute-start | bytes 393224 | tf_op jit(solution)/shard_map/ppermute | solution.py:153
  38.4 1.3 %collective-permute-start.12 = (f32[4,64,128]{2,1,0:T(8,128)S(1)}, f32[4,64,128]{2,1,0:T(8,128)S(1)}, u32[]{:S(2)}, u32[]{:S(2)}) collective-permute-start(f32[4,64,128]{2,1,0:T(8,128)S(1)} %shard_map.90.a), channel_id=1, source_target_pairs={{0,2},{1,3},{2,0},{3,1},{4,6},{5,7},{6,4},{7,5},{8,10},{9,11},{10,... | collective-permute-start | bytes 393224 | tf_op jit(solution)/shard_map/ppermute | solution.py:153
  41.0 3.7 %collective-permute-start.17 = (bf16[4,64,1024]{2,1,0:T(8,128)(2,1)S(1)}, bf16[4,64,1024]{2,1,0:T(8,128)(2,1)S(1)}, u32[]{:S(2)}, u32[]{:S(2)}) collective-permute-start(bf16[4,64,1024]{2,1,0:T(8,128)(2,1)S(1)} %shard_map.95), channel_id=1, source_target_pairs={{0,24},{4,28},{24,0},{28,4},{1,25},{5,29},{25,1},{29,5},{2,26},{6,... | collective-permute-start | bytes 1572872 | tf_op jit(solution)/shard_map/ppermute | solution.py:153
  47.7 1.6 %collective-permute-start.14 = (f32[8,256]{1,0:T(8,128)S(1)}, f32[8,256]{1,0:T(8,128)S(1)}, u32[]{:S(2)}, u32[]{:S(2)}) collective-permute-start(f32[8,256]{1,0:T(8,128)S(1)} %get-tuple-element.24.stats), channel_id=1, source_target_pairs={{0,25},{1,24},{2,27},{3,26},{4,29},{5,28},{6,31},{7,30},{8,17},{9,... | collective-permute-start | bytes 24584 | tf_op jit(solution)/shard_map/ppermute | solution.py:177
  49.3 8.3 %collective-permute-done.14.far_stats = f32[8,256]{1,0:T(8,128)S(1)} collective-permute-done((f32[8,256]{1,0:T(8,128)S(1)}, f32[8,256]{1,0:T(8,128)S(1)}, u32[]{:S(2)}, u32[]{:S(2)}) %collective-permute-start.14) | collective-permute-done | bytes 8224 | tf_op jit(solution)/shard_map/ppermute | solution.py:177
  58.7 1.8 %collective-permute-start.15 = (bf16[4,64,128]{2,1,0:T(8,128)(2,1)S(1)}, bf16[4,64,128]{2,1,0:T(8,128)(2,1)S(1)}, u32[]{:S(2)}, u32[]{:S(2)}) collective-permute-start(bf16[4,64,128]{2,1,0:T(8,128)(2,1)S(1)} %get-tuple-element.30), channel_id=1, source_target_pairs={{0,24},{4,28},{8,16},{12,20},{16,8},{20,12},{24,0},{28,4},{1,25},{... | collective-permute-start | bytes 196616 | tf_op jit(solution)/shard_map/ppermute | solution.py:153
  60.5 10.9 %collective-permute-start.18 = (bf16[136,1024]{1,0:T(8,128)(2,1)S(1)}, bf16[136,1024]{1,0:T(8,128)(2,1)S(1)}, u32[]{:S(2)}, u32[]{:S(2)}) collective-permute-start(bf16[136,1024]{1,0:T(8,128)(2,1)S(1)} %get-tuple-element.32), channel_id=1, source_target_pairs={{0,12},{4,8},{8,4},{12,0},{16,28},{20,24},{24,20},{28,16},{1,13},{... | collective-permute-start | bytes 835592 | tf_op jit(solution)/shard_map/ppermute | solution.py:153
  71.4 1.5 %collective-permute-start.20 = (bf16[136,1024]{1,0:T(8,128)(2,1)S(1)}, bf16[136,1024]{1,0:T(8,128)(2,1)S(1)}, u32[]{:S(2)}, u32[]{:S(2)}) collective-permute-start(bf16[136,1024]{1,0:T(8,128)(2,1)S(1)} %get-tuple-element.34), channel_id=1, source_target_pairs={{0,4},{4,0},{8,12},{12,8},{16,20},{20,16},{24,28},{28,24},{1,5},{5... | collective-permute-start | bytes 835592 | tf_op jit(solution)/shard_map/ppermute | solution.py:153
  72.9 1.9 %shard_map.94 = (f32[1,256]{1,0:T(1,128)}, f32[256,1024]{1,0:T(8,128)S(1)}, f32[256,1024]{1,0:T(8,128)S(1)}) custom-call(s32[16]{0:T(128)S(1)} %shard_map.85.table, f32[256,256]{1,0:T(8,128)S(1)} %get-tuple-element.23.scores_in, f32[8,256]{1,0:T(8,128)S(1)} %get-tuple-element.24.stats, f32[8,256]{1,0:T(8,128)S(1)} %collective-permute-done.14.far_stats, ...), custom_call_target="tpu_custom_call" | custom-call | tf_op jit(solution)/shard_map/pallas_call | solution.py:443
  74.8 1.9 %shard_map.96 = bf16[256,1024]{1,0:T(8,128)(2,1)} custom-call(s32[16]{0:T(128)S(1)} %shard_map.85.table, f32[256,1024]{1,0:T(8,128)S(1)} %get-tuple-element.29.query_total, bf16[4,64,128]{2,1,0:T(8,128)(2,1)S(1)} %collective-permute-done.15.weights_far, bf16[4,64,1024]{2,1,0:T(8,128)(2,1)S(1)} %collective-permute-done.16.refs_0_, ...), custom_call_target="tpu_custom_call" | custom-call | tf_op jit(solution)/shard_map/pallas_call | solution.py:443
  76.7 2.2 %collective-permute-done.18.refs_0_ = bf16[136,1024]{1,0:T(8,128)(2,1)S(1)} collective-permute-done((bf16[136,1024]{1,0:T(8,128)(2,1)S(1)}, bf16[136,1024]{1,0:T(8,128)(2,1)S(1)}, u32[]{:S(2)}, u32[]{:S(2)}) %collective-permute-start.18) | collective-permute-done | bytes 278560 | tf_op jit(solution)/shard_map/ppermute | solution.py:153
  79.0 5.9 %collective-permute-done.19.refs_1_ = bf16[136,1024]{1,0:T(8,128)(2,1)S(1)} collective-permute-done((bf16[136,1024]{1,0:T(8,128)(2,1)S(1)}, bf16[136,1024]{1,0:T(8,128)(2,1)S(1)}, u32[]{:S(2)}, u32[]{:S(2)}) %collective-permute-start.19) | collective-permute-done | bytes 278560 | tf_op jit(solution)/shard_map/ppermute | solution.py:153
  84.9 1.4 %shard_map.97 = bf16[256,1024]{1,0:T(8,128)(2,1)} custom-call(f32[256,1024]{1,0:T(8,128)S(1)} %get-tuple-element.31.own_part, bf16[136,1024]{1,0:T(8,128)(2,1)S(1)} %collective-permute-done.18.refs_0_, bf16[136,1024]{1,0:T(8,128)(2,1)S(1)} %collective-permute-done.19.refs_1_, bf16[136,1024]{1,0:T(8,128)(2,1)S(1)} %collective-permute-done.20.refs_2_), custom_call_target="tpu_custom_call" | custom-call | tf_op jit(solution)/shard_map/pallas_call | solution.py:443
  (47 shorter events, 9.8 us)
Async XLA Ops:
  0.6 4.2 %copy-start = (bf16[16,16,1024]{2,1,0:T(8,128)(2,1)S(1)}, bf16[16,16,1024]{2,1,0:T(8,128)(2,1)}, u32[]{:S(2)}) copy-start(bf16[16,16,1024]{2,1,0:T(8,128)(2,1)} %refs_0_.3) | copy-start | bytes 1572868
  0.6 11.3 %copy-start.1 = (bf16[256,1024]{1,0:T(8,128)(2,1)S(1)}, bf16[256,1024]{1,0:T(8,128)(2,1)}, u32[]{:S(2)}) copy-start(bf16[256,1024]{1,0:T(8,128)(2,1)} %queries.7) | copy-start | bytes 1572868
  1.7 22.1 %collective-permute-start.7 = (bf16[10,16,1024]{2,1,0:T(8,128)(2,1)S(1)}, bf16[10,16,1024]{2,1,0:T(8,128)(2,1)S(1)}, u32[]{:S(2)}, u32[]{:S(2)}) collective-permute-start(bf16[10,16,1024]{2,1,0:T(8,128)(2,1)S(1)} %slice.6), channel_id=1, source_target_pairs={{0,8},{4,12},{8,0},{12,4},{16,24},{20,28},{24,16},{28,20},{1,9},{5... | collective-permute-start | bytes 983048 | tf_op jit(solution)/shard_map/ppermute | solution.py:153
  4.9 25.3 %collective-permute-start.6 = (bf16[16,16,1024]{2,1,0:T(8,128)(2,1)S(1)}, bf16[16,16,1024]{2,1,0:T(8,128)(2,1)S(1)}, u32[]{:S(2)}, u32[]{:S(2)}) collective-permute-start(bf16[16,16,1024]{2,1,0:T(8,128)(2,1)S(1)} %copy-done), channel_id=1, source_target_pairs={{0,4},{4,0},{8,12},{12,8},{16,20},{20,16},{24,28},{28,24},{1,5},{5... | collective-permute-start | bytes 1572872 | tf_op jit(solution)/shard_map/ppermute | solution.py:153
  7.0 15.2 %collective-permute-start.8 = (bf16[6,16,1024]{2,1,0:T(8,128)(2,1)}, bf16[6,16,1024]{2,1,0:T(8,128)(2,1)S(1)}, u32[]{:S(2)}, u32[]{:S(2)}) collective-permute-start(bf16[6,16,1024]{2,1,0:T(8,128)(2,1)} %slice.7), channel_id=1, source_target_pairs={{0,8},{4,12},{8,0},{12,4},{16,24},{20,28},{24,16},{28,20},{1,9},{5... | collective-permute-start | bytes 589832 | tf_op jit(solution)/shard_map/ppermute | solution.py:153
  8.3 10.7 %collective-permute-start = (s32[8]{0:T(128)S(1)}, s32[8]{0:T(128)S(1)}, u32[]{:S(2)}, u32[]{:S(2)}) collective-permute-start(s32[8]{0:T(128)S(1)} %pad_add_fusion.a), channel_id=1, source_target_pairs={{0,24},{4,28},{8,16},{12,20},{16,8},{20,12},{24,0},{28,4},{1,25},{... | collective-permute-start | bytes 104 | tf_op jit(solution)/shard_map/ppermute | solution.py:153
  11.9 18.2 %collective-permute-start.4 = (bf16[256,1024]{1,0:T(8,128)(2,1)S(1)}, bf16[256,1024]{1,0:T(8,128)(2,1)S(1)}, u32[]{:S(2)}, u32[]{:S(2)}) collective-permute-start(bf16[256,1024]{1,0:T(8,128)(2,1)S(1)} %copy-done.1), channel_id=1, source_target_pairs={{8,16},{12,20},{16,8},{20,12},{9,17},{13,21},{17,9},{21,13},{10,18... | collective-permute-start | bytes 1572872 | tf_op jit(solution)/shard_map/ppermute | solution.py:153
  19.0 16.3 %collective-permute-start.5 = (bf16[256,1024]{1,0:T(8,128)(2,1)S(1)}, bf16[256,1024]{1,0:T(8,128)(2,1)S(1)}, u32[]{:S(2)}, u32[]{:S(2)}) collective-permute-start(bf16[256,1024]{1,0:T(8,128)(2,1)S(1)} %copy-done.1), channel_id=1, source_target_pairs={{0,24},{4,28},{24,0},{28,4},{1,25},{5,29},{25,1},{29,5},{2,26},{6,... | collective-permute-start | bytes 1572872 | tf_op jit(solution)/shard_map/ppermute | solution.py:153
  22.2 2.1 %copy-start.2 = (s32[256]{0:T(256)S(1)}, s32[256]{0:T(256)}, u32[]{:S(2)}) copy-start(s32[256]{0:T(256)} %param.10) | copy-start | bytes 3076
  22.3 7.8 %collective-permute-start.10 = (bf16[6,16,1024]{2,1,0:T(8,128)(2,1)S(1)}, bf16[6,16,1024]{2,1,0:T(8,128)(2,1)S(1)}, u32[]{:S(2)}, u32[]{:S(2)}) collective-permute-start(bf16[6,16,1024]{2,1,0:T(8,128)(2,1)S(1)} %collective-permute-done.8.refs_5_.refs_3_), channel_id=1, source_target_pairs={{0,4},{4,0},{8,12},{12,8},{16,20},{20,16},{24,28},{28,24},{1,5},{5... | collective-permute-start | bytes 589832 | tf_op jit(solution)/shard_map/ppermute | solution.py:153
  23.8 11.5 %collective-permute-start.9 = (bf16[10,16,1024]{2,1,0:T(8,128)(2,1)S(1)}, bf16[10,16,1024]{2,1,0:T(8,128)(2,1)S(1)}, u32[]{:S(2)}, u32[]{:S(2)}) collective-permute-start(bf16[10,16,1024]{2,1,0:T(8,128)(2,1)S(1)} %collective-permute-done.7.refs_4_.refs_2_), channel_id=1, source_target_pairs={{0,4},{4,0},{8,12},{12,8},{16,20},{20,16},{24,28},{28,24},{1,5},{5... | collective-permute-start | bytes 983048 | tf_op jit(solution)/shard_map/ppermute | solution.py:153
  30.1 6.7 %collective-permute-start.1 = (f32[128,256]{1,0:T(8,128)S(1)}, f32[128,256]{1,0:T(8,128)S(1)}, u32[]{:S(2)}, u32[]{:S(2)}) collective-permute-start(f32[128,256]{1,0:T(8,128)S(1)} %get-tuple-element.20), channel_id=1, source_target_pairs={{0,1},{1,0},{2,3},{3,2},{4,5},{5,4},{6,7},{7,6},{8,9},{9,8},{10,11... | collective-permute-start | bytes 393224 | tf_op jit(solution)/shard_map/ppermute | solution.py:153
  36.7 1.7 %collective-permute-start.11 = (f32[4,64,128]{2,1,0:T(8,128)S(1)}, f32[4,64,128]{2,1,0:T(8,128)S(1)}, u32[]{:S(2)}, u32[]{:S(2)}) collective-permute-start(f32[4,64,128]{2,1,0:T(8,128)S(1)} %get-tuple-element.22), channel_id=1, source_target_pairs={{0,1},{1,0},{2,3},{3,2},{4,5},{5,4},{6,7},{7,6},{8,9},{9,8},{10,11... | collective-permute-start | bytes 393224 | tf_op jit(solution)/shard_map/ppermute | solution.py:153
  36.8 7.9 %collective-permute-start.2 = (f32[128,256]{1,0:T(8,128)S(1)}, f32[128,256]{1,0:T(8,128)S(1)}, u32[]{:S(2)}, u32[]{:S(2)}) collective-permute-start(f32[128,256]{1,0:T(8,128)S(1)} %shard_map.87.a), channel_id=1, source_target_pairs={{0,2},{1,3},{2,0},{3,1},{4,6},{5,7},{6,4},{7,5},{8,10},{9,11},{10,... | collective-permute-start | bytes 393224 | tf_op jit(solution)/shard_map/ppermute | solution.py:153
  38.4 7.2 %collective-permute-start.12 = (f32[4,64,128]{2,1,0:T(8,128)S(1)}, f32[4,64,128]{2,1,0:T(8,128)S(1)}, u32[]{:S(2)}, u32[]{:S(2)}) collective-permute-start(f32[4,64,128]{2,1,0:T(8,128)S(1)} %shard_map.90.a), channel_id=1, source_target_pairs={{0,2},{1,3},{2,0},{3,1},{4,6},{5,7},{6,4},{7,5},{8,10},{9,11},{10,... | collective-permute-start | bytes 393224 | tf_op jit(solution)/shard_map/ppermute | solution.py:153
  40.3 34.5 %collective-permute-start.16 = (bf16[4,64,1024]{2,1,0:T(8,128)(2,1)S(1)}, bf16[4,64,1024]{2,1,0:T(8,128)(2,1)S(1)}, u32[]{:S(2)}, u32[]{:S(2)}) collective-permute-start(bf16[4,64,1024]{2,1,0:T(8,128)(2,1)S(1)} %shard_map.95), channel_id=1, source_target_pairs={{8,16},{12,20},{16,8},{20,12},{9,17},{13,21},{17,9},{21,13},{10,18... | collective-permute-start | bytes 1572872 | tf_op jit(solution)/shard_map/ppermute | solution.py:153
  41.0 33.8 %collective-permute-start.17 = (bf16[4,64,1024]{2,1,0:T(8,128)(2,1)S(1)}, bf16[4,64,1024]{2,1,0:T(8,128)(2,1)S(1)}, u32[]{:S(2)}, u32[]{:S(2)}) collective-permute-start(bf16[4,64,1024]{2,1,0:T(8,128)(2,1)S(1)} %shard_map.95), channel_id=1, source_target_pairs={{0,24},{4,28},{24,0},{28,4},{1,25},{5,29},{25,1},{29,5},{2,26},{6,... | collective-permute-start | bytes 1572872 | tf_op jit(solution)/shard_map/ppermute | solution.py:153
  44.7 1.4 %collective-permute-start.3 = (f32[128,256]{1,0:T(8,128)S(1)}, f32[128,256]{1,0:T(8,128)S(1)}, u32[]{:S(2)}, u32[]{:S(2)}) collective-permute-start(f32[128,256]{1,0:T(8,128)S(1)} %shard_map.88.in_half), channel_id=1, source_target_pairs={{0,1},{1,0},{2,3},{3,2},{4,5},{5,4},{6,7},{7,6},{8,9},{9,8},{10,11... | collective-permute-start | bytes 393224 | tf_op jit(solution)/shard_map/ppermute | solution.py:153
  45.6 1.4 %collective-permute-start.13 = (f32[4,64,128]{2,1,0:T(8,128)S(1)}, f32[4,64,128]{2,1,0:T(8,128)S(1)}, u32[]{:S(2)}, u32[]{:S(2)}) collective-permute-start(f32[4,64,128]{2,1,0:T(8,128)S(1)} %shard_map.91.list_half), channel_id=1, source_target_pairs={{0,1},{1,0},{2,3},{3,2},{4,5},{5,4},{6,7},{7,6},{8,9},{9,8},{10,11... | collective-permute-start | bytes 393224 | tf_op jit(solution)/shard_map/ppermute | solution.py:153
  47.7 9.9 %collective-permute-start.14 = (f32[8,256]{1,0:T(8,128)S(1)}, f32[8,256]{1,0:T(8,128)S(1)}, u32[]{:S(2)}, u32[]{:S(2)}) collective-permute-start(f32[8,256]{1,0:T(8,128)S(1)} %get-tuple-element.24.stats), channel_id=1, source_target_pairs={{0,25},{1,24},{2,27},{3,26},{4,29},{5,28},{6,31},{7,30},{8,17},{9,... | collective-permute-start | bytes 24584 | tf_op jit(solution)/shard_map/ppermute | solution.py:177
  58.7 12.8 %collective-permute-start.15 = (bf16[4,64,128]{2,1,0:T(8,128)(2,1)S(1)}, bf16[4,64,128]{2,1,0:T(8,128)(2,1)S(1)}, u32[]{:S(2)}, u32[]{:S(2)}) collective-permute-start(bf16[4,64,128]{2,1,0:T(8,128)(2,1)S(1)} %get-tuple-element.30), channel_id=1, source_target_pairs={{0,24},{4,28},{8,16},{12,20},{16,8},{20,12},{24,0},{28,4},{1,25},{... | collective-permute-start | bytes 196616 | tf_op jit(solution)/shard_map/ppermute | solution.py:153
  60.5 18.5 %collective-permute-start.18 = (bf16[136,1024]{1,0:T(8,128)(2,1)S(1)}, bf16[136,1024]{1,0:T(8,128)(2,1)S(1)}, u32[]{:S(2)}, u32[]{:S(2)}) collective-permute-start(bf16[136,1024]{1,0:T(8,128)(2,1)S(1)} %get-tuple-element.32), channel_id=1, source_target_pairs={{0,12},{4,8},{8,4},{12,0},{16,28},{20,24},{24,20},{28,16},{1,13},{... | collective-permute-start | bytes 835592 | tf_op jit(solution)/shard_map/ppermute | solution.py:153
  71.4 13.5 %collective-permute-start.19 = (bf16[136,1024]{1,0:T(8,128)(2,1)S(1)}, bf16[136,1024]{1,0:T(8,128)(2,1)S(1)}, u32[]{:S(2)}, u32[]{:S(2)}) collective-permute-start(bf16[136,1024]{1,0:T(8,128)(2,1)S(1)} %get-tuple-element.33), channel_id=1, source_target_pairs={{0,8},{4,12},{8,0},{12,4},{16,24},{20,28},{24,16},{28,20},{1,9},{5... | collective-permute-start | bytes 835592 | tf_op jit(solution)/shard_map/ppermute | solution.py:153
  71.4 13.5 %collective-permute-start.20 = (bf16[136,1024]{1,0:T(8,128)(2,1)S(1)}, bf16[136,1024]{1,0:T(8,128)(2,1)S(1)}, u32[]{:S(2)}, u32[]{:S(2)}) collective-permute-start(bf16[136,1024]{1,0:T(8,128)(2,1)S(1)} %get-tuple-element.34), channel_id=1, source_target_pairs={{0,4},{4,0},{8,12},{12,8},{16,20},{20,16},{24,28},{28,24},{1,5},{5... | collective-permute-start | bytes 835592 | tf_op jit(solution)/shard_map/ppermute | solution.py:153
  (2 other events, 1.9 us)

commit v4 on v3

--- a/solution.py
+++ b/solution.py
@@ -142,8 +142,9 @@
         and feature_width % 128 == 0
         and (block_total * shard_rows) % 256 == 0
         and block_total <= 4 * LIVE_MAX
-        and block_total % 8 == 0
+        and block_total % 16 == 0
         and 2 * LIVE_MAX * shard_rows <= feature_width
+        and dp_count > 4
         and LIVE_MAX % 2 == 0
     )
 
@@ -227,6 +228,13 @@
         for side in range(2):
             for s in range(self.slots):
                 yield (side * self.slots + s, side, s) + self.slot(side, s)
+
+
+def cut_kernel(rows, *chunks):
+    first = 0
+    for chunk in chunks:
+        chunk[...] = rows[first : first + chunk.shape[0]]
+        first += chunk.shape[0]
 
 
 def own_scores_kernel(local, queries, _, keep, send):
@@ -424,7 +432,7 @@
         listed = piece[count:, :count][0:1].astype(jnp.float32)
         chosen = jnp.where(same_row & (listed == block), 1.0, 0.0).astype(jnp.bfloat16)
         total = total + dot(chosen, piece[:count])
-    grad_passages[...] = total.astype(jnp.bfloat16)
+    grad_passages[...] = total.astype(grad_passages.dtype)
 
 
 def local_call(kernel, outs, scratch=(), hbm=()):
@@ -470,8 +478,10 @@
         Lists, block_count=block_count, list_cap=list_cap, slots=slots
     )
 
-    cut_at = block_total * 5 // 8
-    chunks = [passages[:cut_at], passages[cut_at:]]
+    cut_at = block_total * 11 // 16
+    chunks = local_call(
+        cut_kernel, [((n, shard_rows, width), bf16) for n in (cut_at, block_total - cut_at)]
+    )(passages)
     by_peer = {0: [passages]}
     for k in sorted(peers, key=lambda k: (k.bit_count(), -k)):
         low = k & -k
@@ -540,9 +550,10 @@
         scratch=[((query_rows, width), f32)],
         hbm=(0,),
     )(table, query_total, weights_far, *borrowed)
-    (grad_passages,) = local_call(
-        functools.partial(collect_kernel, shard_rows), [((own_rows, width), bf16)], hbm=(0,)
-    )(own_part, *returned)
+    collect = functools.partial(collect_kernel, shard_rows)
+    last = returned.pop(1)
+    (own_part,) = local_call(collect, [((own_rows, width), f32)])(own_part, *returned)
+    (grad_passages,) = local_call(collect, [((own_rows, width), bf16)], hbm=(0,))(own_part, last)
     return (
         losses.reshape(query_rows),
         grad_queries,

time: 86.5 us -> 98.6 us (1.14)
  starting transfers between devices: 38 us -> 45.8 us
  Pallas kernels: 10.6 us -> 14.7 us
  waiting for transfers between devices: 33.6 us -> 36.1 us
  local copies, waits for them, and re-layouts: 3.22 us -> 0.78 us
    ppermute x20, starting transfers between devices: 36.4 us -> 44.2 us  [swap(): return lax.ppermute(value, axis, pairs)]
    pallas_call x13 -> x15, Pallas kernels: 10.6 us -> 14.7 us  [call(): pl.pallas_call(kernel, out_shape=shapes, in_specs=[smem if table else vme...]
    ppermute x20, waiting for transfers between devices: 25.2 us -> 27.3 us  [swap(): return lax.ppermute(value, axis, pairs)]
    slice x2 -> x0, local copies, waits for them, and re-layouts: 1.77 us -> none  [mirror_plan(): chunks = [passages[:cut_at], passages[cut_at:]]]
  transfers between devices with their start and end apart: 21 -> 21, of which waited for: 9 -> 8; matrix products, arithmetic and copies ran while one was open for 2% -> 0% of each run, Pallas kernels for 11% -> 13%
where the time goes in v4:
time: 98.6 us; the launch traced here: 98.2 us
  starting transfers between devices  45.8 us (46%)
  waiting for transfers between devices  36.1 us (37%)
  Pallas kernels  14.7 us (15%)
    ppermute x20, starting transfers between devices, swap(): return lax.ppermute(value, axis, pairs)  44.2 us
    ppermute x20, waiting for transfers between devices, swap(): return lax.ppermute(value, axis, pairs)  27.3 us
    pallas_call x15, Pallas kernels, call(): pl.pallas_call(kernel, out_shape=shapes, in_specs=[smem if table else vme...  14.7 us
    ppermute x1, waiting for transfers between devices, swap_shared(): return lax.ppermute(value, ('dp', 'grp'), pairs)  8.74 us
  transfers between devices with their start and end apart: 21, of which 8 were waited for; matrix products, arithmetic and copies ran while one was open for 0% of the time, Pallas kernels for 13%

profile of v4, /device:TPU:0, one launch (start us, length us, event | category | flops | bytes accessed | tf_op | source)
XLA Modules:
  0.0 98.2 jit_solution(17655052880627837147)
XLA Ops:
  0.6 1.1 %shard_map.89 = (bf16[11,16,1024]{2,1,0:T(8,128)(2,1)S(1)}, bf16[5,16,1024]{2,1,0:T(8,128)(2,1)S(1)}) custom-call(bf16[16,16,1024]{2,1,0:T(8,128)(2,1)} %refs_0_.3), custom_call_target="tpu_custom_call" | custom-call | tf_op jit(solution)/shard_map/pallas_call | solution.py:451
  1.8 3.1 %collective-permute-start.7 = (bf16[11,16,1024]{2,1,0:T(8,128)(2,1)S(1)}, bf16[11,16,1024]{2,1,0:T(8,128)(2,1)S(1)}, u32[]{:S(2)}, u32[]{:S(2)}) collective-permute-start(bf16[11,16,1024]{2,1,0:T(8,128)(2,1)S(1)} %get-tuple-element.23), channel_id=1, source_target_pairs={{0,8},{4,12},{8,0},{12,4},{16,24},{20,28},{24,16},{28,20},{1,9},{5... | collective-permute-start | bytes 1081352 | tf_op jit(solution)/shard_map/ppermute | solution.py:154
  5.6 4.4 %collective-permute-start.5 = (bf16[256,1024]{1,0:T(8,128)(2,1)S(1)}, bf16[256,1024]{1,0:T(8,128)(2,1)S(1)}, u32[]{:S(2)}, u32[]{:S(2)}) collective-permute-start(bf16[256,1024]{1,0:T(8,128)(2,1)S(1)} %copy-done), channel_id=1, source_target_pairs={{0,24},{4,28},{24,0},{28,4},{1,25},{5,29},{25,1},{29,5},{2,26},{6,... | collective-permute-start | bytes 1572872 | tf_op jit(solution)/shard_map/ppermute | solution.py:154
  10.0 1.6 %collective-permute-start.6 = (bf16[16,16,1024]{2,1,0:T(8,128)(2,1)}, bf16[16,16,1024]{2,1,0:T(8,128)(2,1)S(1)}, u32[]{:S(2)}, u32[]{:S(2)}) collective-permute-start(bf16[16,16,1024]{2,1,0:T(8,128)(2,1)} %refs_0_.3), channel_id=1, source_target_pairs={{0,4},{4,0},{8,12},{12,8},{16,20},{20,16},{24,28},{28,24},{1,5},{5... | collective-permute-start | bytes 1572872 | tf_op jit(solution)/shard_map/ppermute | solution.py:154
  11.7 1.4 %collective-permute-start = (s32[8]{0:T(128)S(1)}, s32[8]{0:T(128)S(1)}, u32[]{:S(2)}, u32[]{:S(2)}) collective-permute-start(s32[8]{0:T(128)S(1)} %pad_add_fusion.a), channel_id=1, source_target_pairs={{0,24},{4,28},{8,16},{12,20},{16,8},{20,12},{24,0},{28,4},{1,25},{... | collective-permute-start | bytes 104 | tf_op jit(solution)/shard_map/ppermute | solution.py:154
  13.1 13.9 %collective-permute-done.b = s32[8]{0:T(128)S(1)} collective-permute-done((s32[8]{0:T(128)S(1)}, s32[8]{0:T(128)S(1)}, u32[]{:S(2)}, u32[]{:S(2)}) %collective-permute-start) | collective-permute-done | bytes 64 | tf_op jit(solution)/shard_map/ppermute | solution.py:154
  27.0 6.0 %collective-permute-start.8 = (bf16[5,16,1024]{2,1,0:T(8,128)(2,1)S(1)}, bf16[5,16,1024]{2,1,0:T(8,128)(2,1)S(1)}, u32[]{:S(2)}, u32[]{:S(2)}) collective-permute-start(bf16[5,16,1024]{2,1,0:T(8,128)(2,1)S(1)} %get-tuple-element.24), channel_id=1, source_target_pairs={{0,8},{4,12},{8,0},{12,4},{16,24},{20,28},{24,16},{28,20},{1,9},{5... | collective-permute-start | bytes 491528 | tf_op jit(solution)/shard_map/ppermute | solution.py:154
  33.0 1.5 %collective-permute-start.9 = (bf16[11,16,1024]{2,1,0:T(8,128)(2,1)S(1)}, bf16[11,16,1024]{2,1,0:T(8,128)(2,1)S(1)}, u32[]{:S(2)}, u32[]{:S(2)}) collective-permute-start(bf16[11,16,1024]{2,1,0:T(8,128)(2,1)S(1)} %collective-permute-done.7.refs_4_.refs_2_), channel_id=1, source_target_pairs={{0,4},{4,0},{8,12},{12,8},{16,20},{20,16},{24,28},{28,24},{1,5},{5... | collective-permute-start | bytes 1081352 | tf_op jit(solution)/shard_map/ppermute | solution.py:154
  34.4 1.8 %collective-permute-done.8.refs_5_.refs_3_ = bf16[5,16,1024]{2,1,0:T(8,128)(2,1)S(1)} collective-permute-done((bf16[5,16,1024]{2,1,0:T(8,128)(2,1)S(1)}, bf16[5,16,1024]{2,1,0:T(8,128)(2,1)S(1)}, u32[]{:S(2)}, u32[]{:S(2)}) %collective-permute-start.8) | collective-permute-done | bytes 163872 | tf_op jit(solution)/shard_map/ppermute | solution.py:154
  36.2 1.5 %collective-permute-start.10 = (bf16[5,16,1024]{2,1,0:T(8,128)(2,1)S(1)}, bf16[5,16,1024]{2,1,0:T(8,128)(2,1)S(1)}, u32[]{:S(2)}, u32[]{:S(2)}) collective-permute-start(bf16[5,16,1024]{2,1,0:T(8,128)(2,1)S(1)} %collective-permute-done.8.refs_5_.refs_3_), channel_id=1, source_target_pairs={{0,4},{4,0},{8,12},{12,8},{16,20},{20,16},{24,28},{28,24},{1,5},{5... | collective-permute-start | bytes 491528 | tf_op jit(solution)/shard_map/ppermute | solution.py:154
  38.4 1.5 %shard_map.86 = (f32[128,256]{1,0:T(8,128)S(1)}, f32[128,256]{1,0:T(8,128)S(1)}) custom-call(bf16[256,1024]{1,0:T(8,128)(2,1)} %bitcast.local, bf16[256,1024]{1,0:T(8,128)(2,1)S(1)} %copy-done, f32[2,256]{1,0:T(2,128)S(1)} %pad_maximum_fusion._.per_query), custom_call_target="tpu_custom_call" | custom-call | tf_op jit(solution)/shard_map/pallas_call | solution.py:451
  40.0 1.1 %shard_map.85.table = s32[16]{0:T(128)S(1)} custom-call(s32[8]{0:T(128)S(1)} %pad_add_fusion.a, s32[8]{0:T(128)S(1)} %collective-permute-done.b), custom_call_target="tpu_custom_call" | custom-call | tf_op jit(solution)/shard_map/pallas_call | solution.py:451
  41.1 4.3 %collective-permute-done.10.refs_7_.refs_5_ = bf16[5,16,1024]{2,1,0:T(8,128)(2,1)S(1)} collective-permute-done((bf16[5,16,1024]{2,1,0:T(8,128)(2,1)S(1)}, bf16[5,16,1024]{2,1,0:T(8,128)(2,1)S(1)}, u32[]{:S(2)}, u32[]{:S(2)}) %collective-permute-start.10) | collective-permute-done | bytes 163872 | tf_op jit(solution)/shard_map/ppermute | solution.py:154
  45.4 1.9 %shard_map.90 = (f32[4,64,128]{2,1,0:T(8,128)S(1)}, f32[4,64,128]{2,1,0:T(8,128)S(1)}) custom-call(s32[16]{0:T(128)S(1)} %shard_map.85.table, bf16[256,1024]{1,0:T(8,128)(2,1)S(1)} %copy-done, bf16[256,1024]{1,0:T(8,128)(2,1)S(1)} %collective-permute-done.4.refs_0_.near_source, bf16[256,1024]{1,0:T(8,128)(2,1)S(1)} %collective-permute-done.5.refs_1_.far_source, ...), custom_call_target="tpu_custom_call" | custom-call | tf_op jit(solution)/shard_map/pallas_call | solution.py:451
  48.0 1.6 %collective-permute-start.2 = (f32[128,256]{1,0:T(8,128)S(1)}, f32[128,256]{1,0:T(8,128)S(1)}, u32[]{:S(2)}, u32[]{:S(2)}) collective-permute-start(f32[128,256]{1,0:T(8,128)S(1)} %shard_map.87.a), channel_id=1, source_target_pairs={{0,2},{1,3},{2,0},{3,1},{4,6},{5,7},{6,4},{7,5},{8,10},{9,11},{10,... | collective-permute-start | bytes 393224 | tf_op jit(solution)/shard_map/ppermute | solution.py:154
  52.4 4.3 %collective-permute-start.17 = (bf16[4,64,1024]{2,1,0:T(8,128)(2,1)S(1)}, bf16[4,64,1024]{2,1,0:T(8,128)(2,1)S(1)}, u32[]{:S(2)}, u32[]{:S(2)}) collective-permute-start(bf16[4,64,1024]{2,1,0:T(8,128)(2,1)S(1)} %shard_map.96), channel_id=1, source_target_pairs={{0,24},{4,28},{24,0},{28,4},{1,25},{5,29},{25,1},{29,5},{2,26},{6,... | collective-permute-start | bytes 1572872 | tf_op jit(solution)/shard_map/ppermute | solution.py:154
  59.0 1.6 %collective-permute-start.14 = (f32[8,256]{1,0:T(8,128)S(1)}, f32[8,256]{1,0:T(8,128)S(1)}, u32[]{:S(2)}, u32[]{:S(2)}) collective-permute-start(f32[8,256]{1,0:T(8,128)S(1)} %get-tuple-element.28.stats), channel_id=1, source_target_pairs={{0,25},{1,24},{2,27},{3,26},{4,29},{5,28},{6,31},{7,30},{8,17},{9,... | collective-permute-start | bytes 24584 | tf_op jit(solution)/shard_map/ppermute | solution.py:178
  60.6 8.7 %collective-permute-done.14.far_stats = f32[8,256]{1,0:T(8,128)S(1)} collective-permute-done((f32[8,256]{1,0:T(8,128)S(1)}, f32[8,256]{1,0:T(8,128)S(1)}, u32[]{:S(2)}, u32[]{:S(2)}) %collective-permute-start.14) | collective-permute-done | bytes 8224 | tf_op jit(solution)/shard_map/ppermute | solution.py:178
  70.4 2.4 %collective-permute-start.15 = (bf16[4,64,128]{2,1,0:T(8,128)(2,1)S(1)}, bf16[4,64,128]{2,1,0:T(8,128)(2,1)S(1)}, u32[]{:S(2)}, u32[]{:S(2)}) collective-permute-start(bf16[4,64,128]{2,1,0:T(8,128)(2,1)S(1)} %get-tuple-element.34), channel_id=1, source_target_pairs={{0,24},{4,28},{8,16},{12,20},{16,8},{20,12},{24,0},{28,4},{1,25},{... | collective-permute-start | bytes 196616 | tf_op jit(solution)/shard_map/ppermute | solution.py:154
  72.8 10.5 %collective-permute-start.18 = (bf16[136,1024]{1,0:T(8,128)(2,1)S(1)}, bf16[136,1024]{1,0:T(8,128)(2,1)S(1)}, u32[]{:S(2)}, u32[]{:S(2)}) collective-permute-start(bf16[136,1024]{1,0:T(8,128)(2,1)S(1)} %get-tuple-element.36), channel_id=1, source_target_pairs={{0,12},{4,8},{8,4},{12,0},{16,28},{20,24},{24,20},{28,16},{1,13},{... | collective-permute-start | bytes 835592 | tf_op jit(solution)/shard_map/ppermute | solution.py:154
  83.9 2.0 %collective-permute-start.20 = (bf16[136,1024]{1,0:T(8,128)(2,1)S(1)}, bf16[136,1024]{1,0:T(8,128)(2,1)S(1)}, u32[]{:S(2)}, u32[]{:S(2)}) collective-permute-start(bf16[136,1024]{1,0:T(8,128)(2,1)S(1)} %get-tuple-element.38), channel_id=1, source_target_pairs={{0,8},{4,12},{8,0},{12,4},{16,24},{20,28},{24,16},{28,20},{1,9},{5... | collective-permute-start | bytes 835592 | tf_op jit(solution)/shard_map/ppermute | solution.py:154
  85.8 2.6 %shard_map.95 = (f32[1,256]{1,0:T(1,128)}, f32[256,1024]{1,0:T(8,128)S(1)}, f32[256,1024]{1,0:T(8,128)S(1)}) custom-call(s32[16]{0:T(128)S(1)} %shard_map.85.table, f32[256,256]{1,0:T(8,128)S(1)} %get-tuple-element.27.scores_in, f32[8,256]{1,0:T(8,128)S(1)} %get-tuple-element.28.stats, f32[8,256]{1,0:T(8,128)S(1)} %collective-permute-done.14.far_stats, ...), custom_call_target="tpu_custom_call" | custom-call | tf_op jit(solution)/shard_map/pallas_call | solution.py:451
  88.5 1.9 %shard_map.97 = bf16[256,1024]{1,0:T(8,128)(2,1)} custom-call(s32[16]{0:T(128)S(1)} %shard_map.85.table, f32[256,1024]{1,0:T(8,128)S(1)} %get-tuple-element.33.query_total, bf16[4,64,128]{2,1,0:T(8,128)(2,1)S(1)} %collective-permute-done.15.weights_far, bf16[4,64,1024]{2,1,0:T(8,128)(2,1)S(1)} %collective-permute-done.16.refs_0_, ...), custom_call_target="tpu_custom_call" | custom-call | tf_op jit(solution)/shard_map/pallas_call | solution.py:451
  90.9 5.9 %collective-permute-done.19.refs_1_ = bf16[136,1024]{1,0:T(8,128)(2,1)S(1)} collective-permute-done((bf16[136,1024]{1,0:T(8,128)(2,1)S(1)}, bf16[136,1024]{1,0:T(8,128)(2,1)S(1)}, u32[]{:S(2)}, u32[]{:S(2)}) %collective-permute-start.19) | collective-permute-done | bytes 278560 | tf_op jit(solution)/shard_map/ppermute | solution.py:154
  (47 shorter events, 10.8 us)
Async XLA Ops:
  0.6 4.3 %copy-start = (bf16[256,1024]{1,0:T(8,128)(2,1)S(1)}, bf16[256,1024]{1,0:T(8,128)(2,1)}, u32[]{:S(2)}) copy-start(bf16[256,1024]{1,0:T(8,128)(2,1)} %queries.7) | copy-start | bytes 1572868
  1.8 9.8 %copy-start.3 = (s32[2,3]{1,0:T(2,128)S(1)}, s32[2,3]{1,0:T(2,128)}, u32[]{:S(2)}) copy-start(s32[2,3]{1,0:T(2,128)} %param.8) | copy-start | bytes 76
  1.8 9.9 %copy-start.4 = (s32[2]{0:T(128)S(1)}, s32[2]{0:T(128)}, u32[]{:S(2)}) copy-start(s32[2]{0:T(128)} %param.9) | copy-start | bytes 28
  1.8 31.2 %collective-permute-start.7 = (bf16[11,16,1024]{2,1,0:T(8,128)(2,1)S(1)}, bf16[11,16,1024]{2,1,0:T(8,128)(2,1)S(1)}, u32[]{:S(2)}, u32[]{:S(2)}) collective-permute-start(bf16[11,16,1024]{2,1,0:T(8,128)(2,1)S(1)} %get-tuple-element.23), channel_id=1, source_target_pairs={{0,8},{4,12},{8,0},{12,4},{16,24},{20,28},{24,16},{28,20},{1,9},{5... | collective-permute-start | bytes 1081352 | tf_op jit(solution)/shard_map/ppermute | solution.py:154
  4.9 40.5 %collective-permute-start.4 = (bf16[256,1024]{1,0:T(8,128)(2,1)S(1)}, bf16[256,1024]{1,0:T(8,128)(2,1)S(1)}, u32[]{:S(2)}, u32[]{:S(2)}) collective-permute-start(bf16[256,1024]{1,0:T(8,128)(2,1)S(1)} %copy-done), channel_id=1, source_target_pairs={{8,16},{12,20},{16,8},{20,12},{9,17},{13,21},{17,9},{21,13},{10,18... | collective-permute-start | bytes 1572872 | tf_op jit(solution)/shard_map/ppermute | solution.py:154
  5.6 39.8 %collective-permute-start.5 = (bf16[256,1024]{1,0:T(8,128)(2,1)S(1)}, bf16[256,1024]{1,0:T(8,128)(2,1)S(1)}, u32[]{:S(2)}, u32[]{:S(2)}) collective-permute-start(bf16[256,1024]{1,0:T(8,128)(2,1)S(1)} %copy-done), channel_id=1, source_target_pairs={{0,24},{4,28},{24,0},{28,4},{1,25},{5,29},{25,1},{29,5},{2,26},{6,... | collective-permute-start | bytes 1572872 | tf_op jit(solution)/shard_map/ppermute | solution.py:154
  10.0 35.4 %collective-permute-start.6 = (bf16[16,16,1024]{2,1,0:T(8,128)(2,1)}, bf16[16,16,1024]{2,1,0:T(8,128)(2,1)S(1)}, u32[]{:S(2)}, u32[]{:S(2)}) collective-permute-start(bf16[16,16,1024]{2,1,0:T(8,128)(2,1)} %refs_0_.3), channel_id=1, source_target_pairs={{0,4},{4,0},{8,12},{12,8},{16,20},{20,16},{24,28},{28,24},{1,5},{5... | collective-permute-start | bytes 1572872 | tf_op jit(solution)/shard_map/ppermute | solution.py:154
  11.7 15.2 %collective-permute-start = (s32[8]{0:T(128)S(1)}, s32[8]{0:T(128)S(1)}, u32[]{:S(2)}, u32[]{:S(2)}) collective-permute-start(s32[8]{0:T(128)S(1)} %pad_add_fusion.a), channel_id=1, source_target_pairs={{0,24},{4,28},{8,16},{12,20},{16,8},{20,12},{24,0},{28,4},{1,25},{... | collective-permute-start | bytes 104 | tf_op jit(solution)/shard_map/ppermute | solution.py:154
  27.0 9.3 %collective-permute-start.8 = (bf16[5,16,1024]{2,1,0:T(8,128)(2,1)S(1)}, bf16[5,16,1024]{2,1,0:T(8,128)(2,1)S(1)}, u32[]{:S(2)}, u32[]{:S(2)}) collective-permute-start(bf16[5,16,1024]{2,1,0:T(8,128)(2,1)S(1)} %get-tuple-element.24), channel_id=1, source_target_pairs={{0,8},{4,12},{8,0},{12,4},{16,24},{20,28},{24,16},{28,20},{1,9},{5... | collective-permute-start | bytes 491528 | tf_op jit(solution)/shard_map/ppermute | solution.py:154
  33.0 12.5 %collective-permute-start.9 = (bf16[11,16,1024]{2,1,0:T(8,128)(2,1)S(1)}, bf16[11,16,1024]{2,1,0:T(8,128)(2,1)S(1)}, u32[]{:S(2)}, u32[]{:S(2)}) collective-permute-start(bf16[11,16,1024]{2,1,0:T(8,128)(2,1)S(1)} %collective-permute-done.7.refs_4_.refs_2_), channel_id=1, source_target_pairs={{0,4},{4,0},{8,12},{12,8},{16,20},{20,16},{24,28},{28,24},{1,5},{5... | collective-permute-start | bytes 1081352 | tf_op jit(solution)/shard_map/ppermute | solution.py:154
  36.2 9.2 %collective-permute-start.10 = (bf16[5,16,1024]{2,1,0:T(8,128)(2,1)S(1)}, bf16[5,16,1024]{2,1,0:T(8,128)(2,1)S(1)}, u32[]{:S(2)}, u32[]{:S(2)}) collective-permute-start(bf16[5,16,1024]{2,1,0:T(8,128)(2,1)S(1)} %collective-permute-done.8.refs_5_.refs_3_), channel_id=1, source_target_pairs={{0,4},{4,0},{8,12},{12,8},{16,20},{20,16},{24,28},{28,24},{1,5},{5... | collective-permute-start | bytes 491528 | tf_op jit(solution)/shard_map/ppermute | solution.py:154
  45.4 2.5 %collective-permute-start.1 = (f32[128,256]{1,0:T(8,128)S(1)}, f32[128,256]{1,0:T(8,128)S(1)}, u32[]{:S(2)}, u32[]{:S(2)}) collective-permute-start(f32[128,256]{1,0:T(8,128)S(1)} %get-tuple-element.22), channel_id=1, source_target_pairs={{0,1},{1,0},{2,3},{3,2},{4,5},{5,4},{6,7},{7,6},{8,9},{9,8},{10,11... | collective-permute-start | bytes 393224 | tf_op jit(solution)/shard_map/ppermute | solution.py:154
  47.4 2.2 %collective-permute-start.11 = (f32[4,64,128]{2,1,0:T(8,128)S(1)}, f32[4,64,128]{2,1,0:T(8,128)S(1)}, u32[]{:S(2)}, u32[]{:S(2)}) collective-permute-start(f32[4,64,128]{2,1,0:T(8,128)S(1)} %get-tuple-element.26), channel_id=1, source_target_pairs={{0,1},{1,0},{2,3},{3,2},{4,5},{5,4},{6,7},{7,6},{8,9},{9,8},{10,11... | collective-permute-start | bytes 393224 | tf_op jit(solution)/shard_map/ppermute | solution.py:154
  48.0 8.7 %collective-permute-start.2 = (f32[128,256]{1,0:T(8,128)S(1)}, f32[128,256]{1,0:T(8,128)S(1)}, u32[]{:S(2)}, u32[]{:S(2)}) collective-permute-start(f32[128,256]{1,0:T(8,128)S(1)} %shard_map.87.a), channel_id=1, source_target_pairs={{0,2},{1,3},{2,0},{3,1},{4,6},{5,7},{6,4},{7,5},{8,10},{9,11},{10,... | collective-permute-start | bytes 393224 | tf_op jit(solution)/shard_map/ppermute | solution.py:154
  49.6 7.2 %collective-permute-start.12 = (f32[4,64,128]{2,1,0:T(8,128)S(1)}, f32[4,64,128]{2,1,0:T(8,128)S(1)}, u32[]{:S(2)}, u32[]{:S(2)}) collective-permute-start(f32[4,64,128]{2,1,0:T(8,128)S(1)} %shard_map.91.a), channel_id=1, source_target_pairs={{0,2},{1,3},{2,0},{3,1},{4,6},{5,7},{6,4},{7,5},{8,10},{9,11},{10,... | collective-permute-start | bytes 393224 | tf_op jit(solution)/shard_map/ppermute | solution.py:154
  51.6 36.8 %collective-permute-start.16 = (bf16[4,64,1024]{2,1,0:T(8,128)(2,1)S(1)}, bf16[4,64,1024]{2,1,0:T(8,128)(2,1)S(1)}, u32[]{:S(2)}, u32[]{:S(2)}) collective-permute-start(bf16[4,64,1024]{2,1,0:T(8,128)(2,1)S(1)} %shard_map.96), channel_id=1, source_target_pairs={{8,16},{12,20},{16,8},{20,12},{9,17},{13,21},{17,9},{21,13},{10,18... | collective-permute-start | bytes 1572872 | tf_op jit(solution)/shard_map/ppermute | solution.py:154
  52.4 36.1 %collective-permute-start.17 = (bf16[4,64,1024]{2,1,0:T(8,128)(2,1)S(1)}, bf16[4,64,1024]{2,1,0:T(8,128)(2,1)S(1)}, u32[]{:S(2)}, u32[]{:S(2)}) collective-permute-start(bf16[4,64,1024]{2,1,0:T(8,128)(2,1)S(1)} %shard_map.96), channel_id=1, source_target_pairs={{0,24},{4,28},{24,0},{28,4},{1,25},{5,29},{25,1},{29,5},{2,26},{6,... | collective-permute-start | bytes 1572872 | tf_op jit(solution)/shard_map/ppermute | solution.py:154
  56.7 1.4 %collective-permute-start.3 = (f32[128,256]{1,0:T(8,128)S(1)}, f32[128,256]{1,0:T(8,128)S(1)}, u32[]{:S(2)}, u32[]{:S(2)}) collective-permute-start(f32[128,256]{1,0:T(8,128)S(1)} %shard_map.88.in_half), channel_id=1, source_target_pairs={{0,1},{1,0},{2,3},{3,2},{4,5},{5,4},{6,7},{7,6},{8,9},{9,8},{10,11... | collective-permute-start | bytes 393224 | tf_op jit(solution)/shard_map/ppermute | solution.py:154
  56.8 1.5 %collective-permute-start.13 = (f32[4,64,128]{2,1,0:T(8,128)S(1)}, f32[4,64,128]{2,1,0:T(8,128)S(1)}, u32[]{:S(2)}, u32[]{:S(2)}) collective-permute-start(f32[4,64,128]{2,1,0:T(8,128)S(1)} %shard_map.92.list_half), channel_id=1, source_target_pairs={{0,1},{1,0},{2,3},{3,2},{4,5},{5,4},{6,7},{7,6},{8,9},{9,8},{10,11... | collective-permute-start | bytes 393224 | tf_op jit(solution)/shard_map/ppermute | solution.py:154
  59.0 10.3 %collective-permute-start.14 = (f32[8,256]{1,0:T(8,128)S(1)}, f32[8,256]{1,0:T(8,128)S(1)}, u32[]{:S(2)}, u32[]{:S(2)}) collective-permute-start(f32[8,256]{1,0:T(8,128)S(1)} %get-tuple-element.28.stats), channel_id=1, source_target_pairs={{0,25},{1,24},{2,27},{3,26},{4,29},{5,28},{6,31},{7,30},{8,17},{9,... | collective-permute-start | bytes 24584 | tf_op jit(solution)/shard_map/ppermute | solution.py:178
  70.4 13.5 %collective-permute-start.15 = (bf16[4,64,128]{2,1,0:T(8,128)(2,1)S(1)}, bf16[4,64,128]{2,1,0:T(8,128)(2,1)S(1)}, u32[]{:S(2)}, u32[]{:S(2)}) collective-permute-start(bf16[4,64,128]{2,1,0:T(8,128)(2,1)S(1)} %get-tuple-element.34), channel_id=1, source_target_pairs={{0,24},{4,28},{8,16},{12,20},{16,8},{20,12},{24,0},{28,4},{1,25},{... | collective-permute-start | bytes 196616 | tf_op jit(solution)/shard_map/ppermute | solution.py:154
  72.8 18.1 %collective-permute-start.18 = (bf16[136,1024]{1,0:T(8,128)(2,1)S(1)}, bf16[136,1024]{1,0:T(8,128)(2,1)S(1)}, u32[]{:S(2)}, u32[]{:S(2)}) collective-permute-start(bf16[136,1024]{1,0:T(8,128)(2,1)S(1)} %get-tuple-element.36), channel_id=1, source_target_pairs={{0,12},{4,8},{8,4},{12,0},{16,28},{20,24},{24,20},{28,16},{1,13},{... | collective-permute-start | bytes 835592 | tf_op jit(solution)/shard_map/ppermute | solution.py:154
  83.3 13.4 %collective-permute-start.19 = (bf16[136,1024]{1,0:T(8,128)(2,1)S(1)}, bf16[136,1024]{1,0:T(8,128)(2,1)S(1)}, u32[]{:S(2)}, u32[]{:S(2)}) collective-permute-start(bf16[136,1024]{1,0:T(8,128)(2,1)S(1)} %get-tuple-element.37), channel_id=1, source_target_pairs={{0,4},{4,0},{8,12},{12,8},{16,20},{20,16},{24,28},{28,24},{1,5},{5... | collective-permute-start | bytes 835592 | tf_op jit(solution)/shard_map/ppermute | solution.py:154
  83.9 13.3 %collective-permute-start.20 = (bf16[136,1024]{1,0:T(8,128)(2,1)S(1)}, bf16[136,1024]{1,0:T(8,128)(2,1)S(1)}, u32[]{:S(2)}, u32[]{:S(2)}) collective-permute-start(bf16[136,1024]{1,0:T(8,128)(2,1)S(1)} %get-tuple-element.38), channel_id=1, source_target_pairs={{0,8},{4,12},{8,0},{12,4},{16,24},{20,28},{24,16},{28,20},{1,9},{5... | collective-permute-start | bytes 835592 | tf_op jit(solution)/shard_map/ppermute | solution.py:154
  (2 other events, 4.0 us)
